TPU v7x, 256 devices: a whole 4x4x8 slice. The times are simulated.
256 devices in a mesh: gx: 4 (over x), gy: 8 (over z_hi, core), gz: 8 (over z_lo, y).
Axes of the slice: x: 4, y: 4, z: 8 (z_hi: 4, z_lo: 2; z = z_hi * 2 + z_lo), core: 2. Of those that a mesh axis runs over, the one named last changes fastest.
Arguments:
- amplitudes: bfloat16 [131072, 4096], P(('gx', 'gy', 'gz')), may hold values from -6 to 6
- tile_coords: int32 [131072, 2], P(('gx', 'gy', 'gz')), may hold values from 0 to 3149, as said below
- row_slot: int32 [3150], replicated, may hold values from 0 to 3321, as said below
- kc_slot: int32 [3150], replicated, may hold values from 0 to 3192, as said below
- integrals: bfloat16 [3200, 64, 256], P(('gy', 'gz')), may hold values from -0.125 to 0.125
Outputs:
- cycle: bfloat16 [3328, 64, 256], P(('gx', 'gy', 'gz'))
Inputs may be any that keep to these rules, and one draw needn't show every extreme that they name: `tile_coords`: column 0 is a row tile i * 21 + A, column 1 a contraction tile k * 21 + C. A tile's compute device is the device whose gx times the devices along gy plus gy equals row_slot[column 0] // 104, and whose gz equals (kc_slot[column 1] // 50) modulo the devices along gz. At most 4 tiles of one device's list share a compute device; for 32 compute devices every device's list holds exactly 4. `row_slot`: distinct values. Row tiles are dealt to the groups in turn, so the groups' counts differ by at most one, and the row tiles of group g fill the slots from g * 104 upward without gaps. `kc_slot`: distinct values. Contraction tiles are dealt to the groups along gz in turn; the m-th tile of a group has slot (m // 50) * 50 * (devices along gz) + group * 50 + m % 50.
All inputs are finite; a program needn't handle non-finite values.
Results may differ from a plain program's by a relative error of at most 0.013.
Values may be sent and summed in bfloat16 or wider, within the bound.
No kernel may reach another device: no remote copies, remote signals or barrier semaphores. Data moves between devices by JAX's collectives and lax.ppermute only.
A program may use at most 192 MiB of HBM per device.

v0:
```python
import math

import jax
import jax.numpy as jnp
from jax import lax
from jax.sharding import PartitionSpec as P

NOCC = 150
NVT = 21


def body(amplitudes, tile_coords, row_slot, kc_slot, integrals):
    row_groups = lax.axis_size("gx") * lax.axis_size("gy")
    kc_groups = lax.axis_size("gz")
    devices = row_groups * kc_groups
    tile_count = amplitudes.shape[0]
    kc_piece = integrals.shape[0]
    tile_edge = integrals.shape[1]
    columns = integrals.shape[2]
    kc_local = kc_piece * lax.axis_size("gy")
    row_local = (NOCC * NVT + devices - 1) // devices * kc_groups
    capacity = (2 * tile_count + devices - 1) // devices
    row_pos = jnp.take(row_slot, tile_coords[:, 0])
    kc_pos = jnp.take(kc_slot, tile_coords[:, 1])
    row_group = row_pos // row_local
    kc_target = kc_pos // kc_piece % kc_groups
    kc_row = kc_pos // (kc_groups * kc_piece) * kc_piece + kc_pos % kc_piece
    slot_place = row_pos % row_local * kc_local + kc_row
    target = row_group * kc_groups + kc_target
    list_ids = jnp.arange(tile_count, dtype=jnp.int32)
    same_target = (target[:, None] == target[None, :]) & (list_ids[None, :] < list_ids[:, None])
    slot_rank = jnp.sum(same_target.astype(jnp.int32), axis=1)
    send_index = target * capacity + slot_rank
    send_ids = jnp.arange(devices * capacity, dtype=jnp.int32)
    matches = send_ids[:, None] == send_index[None, :]
    present = jnp.any(matches, axis=1)
    source = jnp.sum(jnp.where(matches, list_ids[None, :], 0), axis=1)
    send_tiles = jnp.where(
        present[:, None], jnp.take(amplitudes, source, axis=0), jnp.zeros((), amplitudes.dtype)
    )
    send_place = jnp.where(present, jnp.take(slot_place, source), -1)
    send_tiles = send_tiles.reshape(row_groups, kc_groups, capacity, tile_edge * tile_edge)
    send_place = send_place.reshape(row_groups, kc_groups, capacity)
    got_tiles, got_place = (
        lax.all_to_all(
            lax.all_to_all(send_tiles, ("gx", "gy"), split_axis=0, concat_axis=0, tiled=True),
            "gz",
            split_axis=1,
            concat_axis=1,
            tiled=True,
        ),
        lax.all_to_all(
            lax.all_to_all(send_place, ("gx", "gy"), split_axis=0, concat_axis=0, tiled=True),
            "gz",
            split_axis=1,
            concat_axis=1,
            tiled=True,
        ),
    )
    slab_block = lax.all_gather(integrals, "gy", axis=0, tiled=True)
    slot_total = devices * capacity
    block_rows = math.gcd(slot_total, 128)
    got_tiles = got_tiles.reshape(slot_total, tile_edge, tile_edge)
    got_place = got_place.reshape(slot_total)
    row_ids = jnp.arange(row_local, dtype=jnp.int32)

    def add_tiles(partial_value, part_tiles, part_place):
        safe_place = jnp.maximum(part_place, 0)
        chosen = jnp.take(slab_block, safe_place % kc_local, axis=0)
        product = jnp.einsum("nac,ncj->naj", part_tiles, chosen, preferred_element_type=jnp.float32)
        selector = (
            (row_ids[:, None] == (safe_place // kc_local)[None, :]) & (part_place >= 0)[None, :]
        ).astype(jnp.float32)
        added = jnp.dot(
            selector,
            product.reshape(product.shape[0], tile_edge * columns),
            precision=lax.Precision.HIGHEST,
            preferred_element_type=jnp.float32,
        )
        return partial_value + added.reshape(row_local, tile_edge, columns)

    partial_value = jnp.zeros((row_local, tile_edge, columns), jnp.float32)

    def every_block(block_step, running):
        part_tiles = lax.dynamic_slice_in_dim(got_tiles, block_step * block_rows, block_rows, 0)
        part_place = lax.dynamic_slice_in_dim(got_place, block_step * block_rows, block_rows, 0)
        return add_tiles(running, part_tiles, part_place)

    partial_value = lax.fori_loop(0, slot_total // block_rows, every_block, partial_value)
    summed = lax.psum_scatter(
        partial_value.astype(jnp.bfloat16), "gz", scatter_dimension=0, tiled=True
    )
    return summed


def solution(mesh):
    placed = (
        P(("gx", "gy", "gz"), None),
        P(("gx", "gy", "gz"), None),
        P(),
        P(),
        P(("gy", "gz"), None, None),
    )
    return jax.shard_map(
        body,
        mesh=mesh,
        in_specs=placed,
        out_specs=P(("gx", "gy", "gz"), None, None),
        check_vma=False,
    )
```

profile of v0, /device:TPU:2, one launch (start us, length us, event | category | flops | bytes accessed | tf_op | source)
XLA Modules:
  0.0 915.2 jit_solution(8880678315510757400)
XLA Ops:
  23.1 11.6 %all-to-all-start = ((s32[32,8,4]{1,2,0:T(4,128)}), s32[32,8,4]{1,2,0:T(4,128)S(1)}, u32[]{:S(2)}, u32[]{:S(2)}) async-start(s32[32,8,4]{1,2,0:T(4,128)} %copy.27), calls=%async_computation | async-start | bytes 131072 | tf_op jit(solution)/shard_map/all_to_all | solution.py:53
  34.7 17.8 %gather_fusion.2 = bf16[1024,4096]{1,0:T(8,128)(2,1)} fusion(bf16[512,4096]{1,0:T(8,128)(2,1)} %param.9, s32[1024]{0:T(1024)S(1)} %broadcast_clamp_fusion), kind=kCustom, calls=%fused_computation.4 | custom fusion | bytes 16781312 | tf_op jit(solution)/shard_map/jit(_take)/gather | solution.py:39
  52.5 13.1 %gather.29 = bf16[32,8,4,4096]{3,2,1,0:T(4,128)(2,1)} reshape(bf16[1024,4096]{1,0:T(8,128)(2,1)} %gather_fusion.2) | data formatting | bytes 16777216 | tf_op jit(solution)/shard_map/jit(_take)/gather | solution.py:39
  74.2 9.8 %all-to-all-start.2 = ((bf16[32,8,4,4096]{3,2,1,0:T(4,128)(2,1)}), bf16[32,8,4,4096]{3,2,1,0:T(4,128)(2,1)}, u32[]{:S(2)}, u32[]{:S(2)}) async-start(bf16[32,8,4,4096]{3,2,1,0:T(4,128)(2,1)} %select_select_fusion), calls=%async_computation.2 | async-start | bytes 16777216 | tf_op jit(solution)/shard_map/all_to_all | solution.py:46
  85.5 265.9 %all-to-all-done.2 = bf16[32,8,4,4096]{3,2,1,0:T(4,128)(2,1)} async-done(((bf16[32,8,4,4096]{3,2,1,0:T(4,128)(2,1)}), bf16[32,8,4,4096]{3,2,1,0:T(4,128)(2,1)}, u32[]{:S(2)}, u32[]{:S(2)}) %all-to-all-start.2) | async-done | bytes 8388640 | tf_op jit(solution)/shard_map/all_to_all | solution.py:46
  376.8 92.5 %all-to-all-done.3 = bf16[32,8,4,4096]{3,2,0,1:T(4,128)(2,1)} async-done(((bf16[32,8,4,4096]{3,2,0,1:T(4,128)(2,1)}), bf16[32,8,4,4096]{3,2,0,1:T(4,128)(2,1)}, u32[]{:S(2)}, u32[]{:S(2)}) %all-to-all-start.3) | async-done | bytes 8388640 | tf_op jit(solution)/shard_map/all_to_all | solution.py:45
  477.8 24.2 %reshape.77 = bf16[1024,64,64]{2,1,0:T(8,128)(2,1)} reshape(bf16[32,8,4,4096]{3,2,1,0:T(4,128)(2,1)} %copy.31) | data formatting | bytes 16777216 | tf_op jit(solution)/shard_map/reshape | solution.py:63
  502.0 347.2 %while.16 = (s32[]{:T(128)}, f32[104,64,256]{2,0,1:T(8,128)}, s32[1024]{0:T(1024)S(1)}, bf16[1024,64,64]{2,1,0:T(8,128)(2,1)}, bf16[400,64,256]{2,1,0:T(8,128)(2...) while((s32[]{:T(128)}, f32[104,64,256]{2,0,1:T(8,128)}, s32[1024]{0:T(1024)S(1)}, ...), condition=%wide.region_4.6_spmd.clone, body=%wide.region_3.5_spmd.clone.sunk | while | flops 2891216896 | bytes 78651552 | solution.py:89
  513.7 9.7 %copy.38 = f32[16,8,64,256]{3,1,2,0:T(8,128)} copy(f32[16,8,64,256]{3,2,1,0:T(8,128)S(1)} %bitcast.26) | data formatting | bytes 16777216 | tf_op jit(solution)/shard_map/while
  532.5 11.1 %select_add_fusion.2 = f32[104,64,256]{2,0,1:T(8,128)} fusion(f32[104,64,256]{2,0,1:T(8,128)} %get-tuple-element.250, pred[]{:T(512)S(6)} %compare.4, f32[64,256,128]{2,1,0:T(8,128)} %bitcast.25, s32[128]{0:T(128)S(1)} %and_select_fusion.5, pred[128]{0:T(512)(128)(4,1)S(1)} %get-tuple-element.239), kind=kOutput, calls=%fused_computation.6.clone.1 | convolution fusion | flops 2620680192 | bytes 22020736 | tf_op jit(solution)/shard_map/while/body/eval_jaxpr/dot_general | solution.py:74
  555.4 9.7 %copy.38 = f32[16,8,64,256]{3,1,2,0:T(8,128)} copy(f32[16,8,64,256]{3,2,1,0:T(8,128)S(1)} %bitcast.26) | data formatting | bytes 16777216 | tf_op jit(solution)/shard_map/while
  574.2 13.1 %select_add_fusion.2 = f32[104,64,256]{2,0,1:T(8,128)} fusion(f32[104,64,256]{2,0,1:T(8,128)} %get-tuple-element.250, pred[]{:T(512)S(6)} %compare.4, f32[64,256,128]{2,1,0:T(8,128)} %bitcast.25, s32[128]{0:T(128)S(1)} %and_select_fusion.5, pred[128]{0:T(512)(128)(4,1)S(1)} %get-tuple-element.239), kind=kOutput, calls=%fused_computation.6.clone.1 | convolution fusion | flops 2620680192 | bytes 22020736 | tf_op jit(solution)/shard_map/while/body/eval_jaxpr/dot_general | solution.py:74
  599.0 9.7 %copy.38 = f32[16,8,64,256]{3,1,2,0:T(8,128)} copy(f32[16,8,64,256]{3,2,1,0:T(8,128)S(1)} %bitcast.26) | data formatting | bytes 16777216 | tf_op jit(solution)/shard_map/while
  617.8 13.1 %select_add_fusion.2 = f32[104,64,256]{2,0,1:T(8,128)} fusion(f32[104,64,256]{2,0,1:T(8,128)} %get-tuple-element.250, pred[]{:T(512)S(6)} %compare.4, f32[64,256,128]{2,1,0:T(8,128)} %bitcast.25, s32[128]{0:T(128)S(1)} %and_select_fusion.5, pred[128]{0:T(512)(128)(4,1)S(1)} %get-tuple-element.239), kind=kOutput, calls=%fused_computation.6.clone.1 | convolution fusion | flops 2620680192 | bytes 22020736 | tf_op jit(solution)/shard_map/while/body/eval_jaxpr/dot_general | solution.py:74
  642.6 9.7 %copy.38 = f32[16,8,64,256]{3,1,2,0:T(8,128)} copy(f32[16,8,64,256]{3,2,1,0:T(8,128)S(1)} %bitcast.26) | data formatting | bytes 16777216 | tf_op jit(solution)/shard_map/while
  661.5 13.1 %select_add_fusion.2 = f32[104,64,256]{2,0,1:T(8,128)} fusion(f32[104,64,256]{2,0,1:T(8,128)} %get-tuple-element.250, pred[]{:T(512)S(6)} %compare.4, f32[64,256,128]{2,1,0:T(8,128)} %bitcast.25, s32[128]{0:T(128)S(1)} %and_select_fusion.5, pred[128]{0:T(512)(128)(4,1)S(1)} %get-tuple-element.239), kind=kOutput, calls=%fused_computation.6.clone.1 | convolution fusion | flops 2620680192 | bytes 22020736 | tf_op jit(solution)/shard_map/while/body/eval_jaxpr/dot_general | solution.py:74
  686.3 9.7 %copy.38 = f32[16,8,64,256]{3,1,2,0:T(8,128)} copy(f32[16,8,64,256]{3,2,1,0:T(8,128)S(1)} %bitcast.26) | data formatting | bytes 16777216 | tf_op jit(solution)/shard_map/while
  705.1 13.1 %select_add_fusion.2 = f32[104,64,256]{2,0,1:T(8,128)} fusion(f32[104,64,256]{2,0,1:T(8,128)} %get-tuple-element.250, pred[]{:T(512)S(6)} %compare.4, f32[64,256,128]{2,1,0:T(8,128)} %bitcast.25, s32[128]{0:T(128)S(1)} %and_select_fusion.5, pred[128]{0:T(512)(128)(4,1)S(1)} %get-tuple-element.239), kind=kOutput, calls=%fused_computation.6.clone.1 | convolution fusion | flops 2620680192 | bytes 22020736 | tf_op jit(solution)/shard_map/while/body/eval_jaxpr/dot_general | solution.py:74
  729.9 9.7 %copy.38 = f32[16,8,64,256]{3,1,2,0:T(8,128)} copy(f32[16,8,64,256]{3,2,1,0:T(8,128)S(1)} %bitcast.26) | data formatting | bytes 16777216 | tf_op jit(solution)/shard_map/while
  748.7 13.1 %select_add_fusion.2 = f32[104,64,256]{2,0,1:T(8,128)} fusion(f32[104,64,256]{2,0,1:T(8,128)} %get-tuple-element.250, pred[]{:T(512)S(6)} %compare.4, f32[64,256,128]{2,1,0:T(8,128)} %bitcast.25, s32[128]{0:T(128)S(1)} %and_select_fusion.5, pred[128]{0:T(512)(128)(4,1)S(1)} %get-tuple-element.239), kind=kOutput, calls=%fused_computation.6.clone.1 | convolution fusion | flops 2620680192 | bytes 22020736 | tf_op jit(solution)/shard_map/while/body/eval_jaxpr/dot_general | solution.py:74
  773.6 9.7 %copy.38 = f32[16,8,64,256]{3,1,2,0:T(8,128)} copy(f32[16,8,64,256]{3,2,1,0:T(8,128)S(1)} %bitcast.26) | data formatting | bytes 16777216 | tf_op jit(solution)/shard_map/while
  792.4 13.1 %select_add_fusion.2 = f32[104,64,256]{2,0,1:T(8,128)} fusion(f32[104,64,256]{2,0,1:T(8,128)} %get-tuple-element.250, pred[]{:T(512)S(6)} %compare.4, f32[64,256,128]{2,1,0:T(8,128)} %bitcast.25, s32[128]{0:T(128)S(1)} %and_select_fusion.5, pred[128]{0:T(512)(128)(4,1)S(1)} %get-tuple-element.239), kind=kOutput, calls=%fused_computation.6.clone.1 | convolution fusion | flops 2620680192 | bytes 22020736 | tf_op jit(solution)/shard_map/while/body/eval_jaxpr/dot_general | solution.py:74
  836.0 13.1 %select_add_fusion.2 = f32[104,64,256]{2,0,1:T(8,128)} fusion(f32[104,64,256]{2,0,1:T(8,128)} %get-tuple-element.250, pred[]{:T(512)S(6)} %compare.4, f32[64,256,128]{2,1,0:T(8,128)} %bitcast.25, s32[128]{0:T(128)S(1)} %and_select_fusion.5, pred[128]{0:T(512)(128)(4,1)S(1)} %get-tuple-element.239), kind=kOutput, calls=%fused_computation.6.clone.1 | convolution fusion | flops 2620680192 | bytes 22020736 | tf_op jit(solution)/shard_map/while/body/eval_jaxpr/dot_general | solution.py:74
  855.7 52.6 %reduce-scatter.2.cloned.1.call-done = bf16[13,64,256]{2,1,0:T(8,128)(2,1)} async-done(((bf16[104,64,256]{2,1,0:T(8,128)(2,1)}), bf16[13,64,256]{2,1,0:T(8,128)(2,1)}) %reduce-scatter.2.cloned.1.call-update) | async-done | bytes 426000 | tf_op jit(solution)/shard_map/reduce_scatter | solution.py:90
  (94 shorter events, 243.2 us)
Async XLA Ops:
  6.5 0.8 copy-start
  23.1 51.1 %all-to-all-start = ((s32[32,8,4]{1,2,0:T(4,128)}), s32[32,8,4]{1,2,0:T(4,128)S(1)}, u32[]{:S(2)}, u32[]{:S(2)}) async-start(s32[32,8,4]{1,2,0:T(4,128)} %copy.27), calls=%async_computation | async-start | bytes 131072 | tf_op jit(solution)/shard_map/all_to_all | solution.py:53
  74.2 277.2 %all-to-all-start.2 = ((bf16[32,8,4,4096]{3,2,1,0:T(4,128)(2,1)}), bf16[32,8,4,4096]{3,2,1,0:T(4,128)(2,1)}, u32[]{:S(2)}, u32[]{:S(2)}) async-start(bf16[32,8,4,4096]{3,2,1,0:T(4,128)(2,1)} %select_select_fusion), calls=%async_computation.2 | async-start | bytes 16777216 | tf_op jit(solution)/shard_map/all_to_all | solution.py:46
  84.0 417.9 %all-gather.2.cloned.1.call-start = ((), (), s32[]{:S(2)}) async-start(), calls=%async_computation.5 | async-start | bytes 14745600 | tf_op jit(solution)/shard_map/all_gather | solution.py:60
  351.4 17.7 %all-to-all-start.1 = ((s32[8,1,128]{2,1,0:T(1,128)}), s32[8,1,128]{2,1,0:T(1,128)S(1)}, u32[]{:S(2)}, u32[]{:S(2)}) async-start(s32[8,1,128]{2,1,0:T(1,128)} %reshape.129), calls=%async_computation.1 | async-start | bytes 8192 | tf_op jit(solution)/shard_map/all_to_all | solution.py:52
  369.1 100.2 %all-to-all-start.3 = ((bf16[32,8,4,4096]{3,2,0,1:T(4,128)(2,1)}), bf16[32,8,4,4096]{3,2,0,1:T(4,128)(2,1)}, u32[]{:S(2)}, u32[]{:S(2)}) async-start(bf16[32,8,4,4096]{3,2,0,1:T(4,128)(2,1)} %copy.30), calls=%async_computation.3 | async-start | bytes 16777216 | tf_op jit(solution)/shard_map/all_to_all | solution.py:45
  375.2 533.1 %reduce-scatter.2.cloned.1.call-start = ((), (), s32[]{:S(2)}) async-start(), calls=%async_computation.6 | async-start | bytes 3833856 | tf_op jit(solution)/shard_map/reduce_scatter | solution.py:90
  849.1 59.2 %copy-start.1 = (s32[3150]{0:T(1024)S(1)}, s32[3150]{0:T(1024)}, u32[]{:S(2)}) copy-start(s32[3150]{0:T(1024)} %param.11) | copy-start | bytes 37804
Sparse Core Ops, SparseCore 0:
  86.7 290.4 all-gather.1
  855.8 52.4 reduce-scatter.1
where the time goes:
time: 919 us; the launch traced here: 915 us
  waiting for transfers between devices  412 us (45%)
  local copies, waits for them, and re-layouts  306 us (33%)
  matrix products  136 us (15%)
  starting transfers between devices  36.8 us (4%)
  between operations  13.6 us (1%)
  other arithmetic  11.6 us (1%)
    all_to_all x1, waiting for transfers between devices, body(): lax.all_to_all(send_tiles, ('gx', 'gy'), split_axis=0, concat_axis=0, til...  266 us
    dot_general x8, matrix products, add_tiles(): jnp.dot(selector, product.reshape(product.shape[0], tile_edge * columns),...  103 us
    all_to_all x1, waiting for transfers between devices, body(): lax.all_to_all(lax.all_to_all(send_tiles, ('gx', 'gy'), split_axis=0, con...  92.5 us
    while x8, local copies, waits for them, and re-layouts  77.6 us
    dot_general x8, local copies, waits for them, and re-layouts, add_tiles(): jnp.dot(selector, product.reshape(product.shape[0], tile_edge * columns),...  72.2 us
    gather x8, local copies, waits for them, and re-layouts, add_tiles(): chosen = jnp.take(slab_block, safe_place % kc_local, axis=0)  60 us
    reduce_scatter x1, waiting for transfers between devices, body(): lax.psum_scatter(partial_value.astype(jnp.bfloat16), 'gz', scatter_dimens...  52.6 us
    dot_general x8, matrix products, add_tiles(): jnp.einsum('nac,ncj->naj', part_tiles, chosen, preferred_element_type=jnp...  33 us
  transfers between devices with their start and end apart: 6, of which 3 were waited for; matrix products, arithmetic and copies ran while one was open for 9% of the time, Pallas kernels for 0%

commit v1 on v0

v1 whole, which is shorter than its diff:
```python
import functools

import jax
import jax.numpy as jnp
from jax import lax
from jax.experimental import pallas as pl
from jax.experimental.pallas import tpu as pltpu
from jax.sharding import Mesh, PartitionSpec as P

ALL = ("gx", "zhi", "core", "gz")
GY = ("zhi", "core")
CAP = 4
CHUNKS = (3, 1)
VMEM_LIMIT = 62 * 1024 * 1024


def _relayout_kernel(src_ref, x_ref, out_ref, y_ref, tmp):
    tiles = x_ref.shape[0]
    q_rows = x_ref.shape[1] // 128
    span = 8 * q_rows

    @pl.when(pl.program_id(0) == 0)
    def _():
        def one(g, carry):
            v = x_ref[pl.ds(pl.multiple_of(g * 8, 8), 8), :].astype(jnp.float32)
            for q in range(q_rows):
                tmp[pl.ds(q, 8, stride=q_rows), :] = v[:, q * 128:(q + 1) * 128]
            y_ref[pl.ds(pl.multiple_of(g * span, span), span), :] = tmp[...].astype(y_ref.dtype)
            return carry

        lax.fori_loop(0, tiles // 8, one, 0, unroll=2)

    _copy_slots(src_ref, y_ref, out_ref, q_rows)


def _copy_slots(src_ref, y_ref, out_ref, q_rows):
    slots = out_ref.shape[0] // q_rows
    base = pl.program_id(0) * slots

    def one(s, carry):
        n = src_ref[base + s]
        out_ref[pl.ds(pl.multiple_of(s * q_rows, q_rows), q_rows), :] = y_ref[
            pl.ds(pl.multiple_of(n * q_rows, q_rows), q_rows), :
        ]
        return carry

    lax.fori_loop(0, slots, one, 0, unroll=16)


def _copy_kernel(src_ref, y_ref, held_ref, out_ref, kept_ref):
    _copy_slots(src_ref, y_ref, out_ref, 32)


def first_send(src, x, block):
    tiles, width = x.shape
    q_rows = width // 128
    slots = src.shape[0]
    return pl.pallas_call(
        _relayout_kernel,
        grid_spec=pltpu.PrefetchScalarGridSpec(
            num_scalar_prefetch=1,
            grid=(slots // block,),
            in_specs=[pl.BlockSpec((tiles, width), lambda i, s: (0, 0))],
            out_specs=[
                pl.BlockSpec((block * q_rows, 128), lambda i, s: (i, 0)),
                pl.BlockSpec((tiles * q_rows, 128), lambda i, s: (0, 0)),
            ],
            scratch_shapes=[pltpu.VMEM((8 * q_rows, 128), jnp.float32)],
        ),
        out_shape=[
            jax.ShapeDtypeStruct((slots * q_rows, 128), x.dtype),
            jax.ShapeDtypeStruct((tiles * q_rows, 128), x.dtype),
        ],
        compiler_params=pltpu.CompilerParams(vmem_limit_bytes=VMEM_LIMIT),
        name="first_send",
    )(src, x)


def next_send(src, y, held, block):
    rows = y.shape[0]
    slots = src.shape[0]
    return pl.pallas_call(
        _copy_kernel,
        grid_spec=pltpu.PrefetchScalarGridSpec(
            num_scalar_prefetch=1,
            grid=(slots // block,),
            in_specs=[
                pl.BlockSpec((rows, 128), lambda i, s: (0, 0)),
                pl.BlockSpec(memory_space=pl.ANY),
            ],
            out_specs=[
                pl.BlockSpec((block * 32, 128), lambda i, s: (i, 0)),
                pl.BlockSpec(memory_space=pl.ANY),
            ],
        ),
        out_shape=[
            jax.ShapeDtypeStruct((slots * 32, 128), y.dtype),
            jax.ShapeDtypeStruct(held.shape, held.dtype),
        ],
        input_output_aliases={2: 1},
        compiler_params=pltpu.CompilerParams(vmem_limit_bytes=VMEM_LIMIT),
        name="next_send",
    )(src, y, held)


def _product_kernel(has_in, last, unroll, place_ref, x_ref, w_hbm, *rest):
    if has_in:
        acc_in, out_ref, acc, wbuf, prod, sem = rest
    else:
        out_ref, acc, wbuf, prod, sem = rest
    step = pl.program_id(0)
    edge = 64
    out_rows = out_ref.shape[0]

    @pl.when(step == 0)
    def _():
        copy = pltpu.make_async_copy(w_hbm, wbuf, sem.at[0])
        copy.start()
        if has_in:
            back = pltpu.make_async_copy(acc_in, acc.at[pl.ds(0, out_rows), :], sem.at[1])
            back.start()
            back.wait()
        else:
            acc[...] = jnp.zeros_like(acc)
        copy.wait()

    block = x_ref.shape[0] // 32
    base = step * block

    def group(i, carry):
        rows = []
        for u in range(unroll):
            n = i * unroll + u
            v = place_ref[base + n]
            row = lax.shift_right_logical(v, 10)
            kc = lax.bitwise_and(v, 1023)
            rows.append(row)
            p = x_ref[pl.ds(pl.multiple_of(n * 32, 32), 32), :]
            a = jnp.concatenate([p[:, :64], p[:, 64:]], axis=0)
            w = jnp.concatenate(
                [wbuf[pl.ds(pl.multiple_of((kc + 400 * k) * 16, 16), 16), :] for k in range(4)], axis=0
            )
            prod[u] = jnp.dot(a, w, preferred_element_type=jnp.float32)
        for u in range(unroll):
            where = pl.ds(pl.multiple_of(rows[u] * edge, edge), edge)
            acc[where, :] += prod[u]
        return carry

    lax.fori_loop(0, block // unroll, group, 0)

    @pl.when(step == pl.num_programs(0) - 1)
    def _():
        if last:
            out_ref[...] = acc[pl.ds(0, out_rows), :].astype(out_ref.dtype)
        else:
            away = pltpu.make_async_copy(acc.at[pl.ds(0, out_rows), :], out_ref, sem.at[1])
            away.start()
            away.wait()


def products(place, x, w, acc_in, row_local, last, block=64, unroll=8):
    tiles = place.shape[0]
    has_in = acc_in is not None
    rows = row_local * 64
    operands = (place, x, w) + ((acc_in,) if has_in else ())
    return pl.pallas_call(
        functools.partial(_product_kernel, has_in, last, unroll),
        grid_spec=pltpu.PrefetchScalarGridSpec(
            num_scalar_prefetch=1,
            grid=(tiles // block,),
            in_specs=[
                pl.BlockSpec((block * 32, 128), lambda i, s: (i, 0)),
                pl.BlockSpec(memory_space=pl.ANY),
            ] + ([pl.BlockSpec(memory_space=pl.ANY)] if has_in else []),
            out_specs=pl.BlockSpec((rows, 256), lambda i, s: (0, 0)) if last
            else pl.BlockSpec(memory_space=pl.ANY),
            scratch_shapes=[
                pltpu.VMEM((rows + 64, 256), jnp.float32),
                pltpu.VMEM(w.shape, w.dtype),
                pltpu.VMEM((unroll, 64, 256), jnp.float32),
                pltpu.SemaphoreType.DMA((2,)),
            ],
        ),
        out_shape=jax.ShapeDtypeStruct((rows, 256), jnp.bfloat16 if last else jnp.float32),
        compiler_params=pltpu.CompilerParams(vmem_limit_bytes=VMEM_LIMIT),
        name="products",
    )(*operands)


def body(amplitudes, tile_coords, row_slot, kc_slot, integrals):
    kc_groups = lax.axis_size("gz")
    planes = lax.axis_size("gx")
    devices = planes * lax.axis_size("zhi") * lax.axis_size("core") * kc_groups
    tile_count = amplitudes.shape[0]
    kc_piece, tile_edge, columns = integrals.shape
    row_local = 104
    gy_size = lax.axis_size("zhi") * lax.axis_size("core")
    part = tile_edge // planes
    quarter = lax.dynamic_slice_in_dim(integrals, lax.axis_index("gx") * part, part, 1)
    quarter = quarter.reshape(kc_piece * part, columns)
    slab = lax.all_gather(quarter, "zhi", axis=0, tiled=True)

    row_pos = jnp.take(row_slot, tile_coords[:, 0])
    kc_pos = jnp.take(kc_slot, tile_coords[:, 1])
    kc_target = kc_pos // kc_piece % kc_groups
    kc_gy = kc_pos // (kc_groups * kc_piece)
    kc_row = kc_gy % 2 * (kc_piece * gy_size // 2) + kc_gy // 2 * kc_piece + kc_pos % kc_piece
    place = row_pos % row_local * 1024 + kc_row
    target = row_pos // row_local * kc_groups + kc_target
    ids = jnp.arange(tile_count, dtype=jnp.int32)
    same = (target[:, None] == target[None, :]) & (ids[None, :] < ids[:, None])
    rank = jnp.sum(same.astype(jnp.int32), axis=1)
    send_index = rank * devices + target
    send_ids = jnp.arange(devices * CAP, dtype=jnp.int32)
    matches = send_ids[:, None] == send_index[None, :]
    source = jnp.sum(jnp.where(matches, ids[None, :], 0), axis=1)
    empty = row_local * 1024
    sent_place = empty + jnp.sum(jnp.where(matches, place[None, :] - empty, 0), axis=1)
    source = source.reshape(CAP, devices)
    sent_place = sent_place.reshape(CAP, devices).T
    got_place = lax.all_to_all(sent_place, ALL, split_axis=0, concat_axis=0, tiled=True)

    acc = None
    start = 0
    relaid = None
    got = []
    for size in CHUNKS:
        src = source[start:start + size].T.reshape(-1)
        if relaid is None:
            sent, relaid = first_send(src, amplitudes, 64)
        else:
            sent, slab = next_send(src, relaid, slab, 64)
            slab = lax.all_gather(slab, ("gx", "core"), axis=0, tiled=True)
        arrived = lax.all_to_all(
            sent.reshape(devices, size * 32, 128), ALL, split_axis=0, concat_axis=0, tiled=True
        )
        got.append((arrived.reshape(devices * size * 32, 128), got_place[:, start:start + size].reshape(-1)))
        start += size
    for index, (tiles, places) in enumerate(got):
        acc = products(places, tiles, slab, acc, row_local, index == len(got) - 1)
    shared = lax.all_to_all(
        acc.reshape(kc_groups, row_local // kc_groups * tile_edge, columns), "gz", split_axis=0, concat_axis=0, tiled=True
    )
    total = jnp.sum(shared.astype(jnp.float32), axis=0).astype(jnp.bfloat16)
    total = total.reshape(row_local // kc_groups, 2, tile_edge // 2, columns)
    return jnp.swapaxes(total, 1, 2).reshape(row_local // kc_groups, tile_edge, columns)


def solution(mesh):
    gx, gy, gz = mesh.devices.shape
    fine = Mesh(mesh.devices.reshape(gx, gy // 2, 2, gz), ALL)
    placed = (
        P(ALL, None),
        P(ALL, None),
        P(),
        P(),
        P(GY + ("gz",), None, None),
    )

    return jax.shard_map(
        body, mesh=fine, in_specs=placed, out_specs=P(ALL, None, None), check_vma=False
    )
```

time: 919 us -> 374 us (0.41)
  waiting for transfers between devices: 412 us -> 36.8 us
  local copies, waits for them, and re-layouts: 306 us -> 13.9 us
  blocking collectives: 0 us -> 218 us
  matrix products: 136 us -> 0 us
  Pallas kernels: 0 us -> 76.2 us
  starting transfers between devices: 36.8 us -> 9.42 us
    all_to_all x4 -> x1, waiting for transfers between devices: 358 us -> 14.6 us  [body(): lax.all_to_all(sent.reshape(devices, size * 32, 128), ALL, split_axis=0,...]
    all_to_all x0 -> x3, blocking collectives: none -> 218 us  [the longest x1 151 us: body(): lax.all_to_all(sent.reshape(devices, size * 32, 128), ALL, split_axis=0,...]
    dot_general x16 -> x0, matrix products: 136 us -> none  [the longest x8 103 us: add_tiles(): jnp.dot(selector, product.reshape(product.shape[0], tile_edge * columns),...]
    gather x12 -> x0, local copies, waits for them, and re-layouts: 98 us -> none  [the longest x8 60 us: add_tiles(): chosen = jnp.take(slab_block, safe_place % kc_local, axis=0)]
    while x9 -> x0, local copies, waits for them, and re-layouts: 84.2 us -> none
    pallas_call x0 -> x4, Pallas kernels: none -> 76.2 us  [the longest x2 55.3 us: products(): pl.pallas_call(functools.partial(_product_kernel, has_in, last, unroll),...]
    dot_general x8 -> x0, local copies, waits for them, and re-layouts: 72.2 us -> none  [add_tiles(): jnp.dot(selector, product.reshape(product.shape[0], tile_edge * columns),...]
    reduce_scatter x1 -> x0, waiting for transfers between devices: 52.6 us -> none  [body(): lax.psum_scatter(partial_value.astype(jnp.bfloat16), 'gz', scatter_dimens...]
  transfers between devices with their start and end apart: 6 -> 3, of which waited for: 3 -> 2; matrix products, arithmetic and copies ran while one was open for 9% -> 3% of each run, Pallas kernels for 0% -> 14%
where the time goes in v1:
time: 374 us; the launch traced here: 372 us
  blocking collectives  218 us (58%)
  Pallas kernels  76.2 us (20%)
  waiting for transfers between devices  36.8 us (10%)
  local copies, waits for them, and re-layouts  13.9 us (4%)
  between operations  13.5 us (4%)
  starting transfers between devices  9.42 us (3%)
    all_to_all x1, blocking collectives, body(): lax.all_to_all(sent.reshape(devices, size * 32, 128), ALL, split_axis=0,...  151 us
    pallas_call x2, Pallas kernels, products(): pl.pallas_call(functools.partial(_product_kernel, has_in, last, unroll),...  55.3 us
    all_to_all x1, blocking collectives, body(): lax.all_to_all(acc.reshape(kc_groups, row_local // kc_groups * tile_edge,...  45.8 us
    all_gather x1, waiting for transfers between devices, body(): slab = lax.all_gather(quarter, 'zhi', axis=0, tiled=True)  22.1 us
    all_to_all x1, blocking collectives, body(): lax.all_to_all(sent_place, ALL, split_axis=0, concat_axis=0, tiled=True)  22 us
    pallas_call x1, Pallas kernels, first_send(): pl.pallas_call(_relayout_kernel, grid_spec=pltpu.PrefetchScalarGridSpec(n...  15.7 us
    all_to_all x1, waiting for transfers between devices, body(): lax.all_to_all(sent.reshape(devices, size * 32, 128), ALL, split_axis=0,...  14.6 us
    all_to_all x1, starting transfers between devices, body(): lax.all_to_all(sent.reshape(devices, size * 32, 128), ALL, split_axis=0,...  9.37 us
  transfers between devices with their start and end apart: 3, of which 2 were waited for; matrix products, arithmetic and copies ran while one was open for 3% of the time, Pallas kernels for 14%

profile of v1, /device:TPU:2, one launch (start us, length us, event | category | flops | bytes accessed | tf_op | source)
XLA Modules:
  0.0 371.8 jit_solution(1434527162914188685)
XLA Ops:
  6.6 1.4 copy-done
  8.0 0.8 constant_dynamic-slice_fusion
  8.8 0.8 fusion.14
  9.6 3.1 gather_fusion
  12.8 3.1 gather_fusion.1
  16.0 0.2 convert_reduce_fusion
  16.2 0.7 select_reduce_fusion
  17.0 0.6 slice.33.src_ref
  17.7 0.8 reshape.62.src_ref
  18.5 15.7 %first_send.1 = (bf16[24576,128]{1,0:T(8,128)(2,1)}, bf16[16384,128]{1,0:T(8,128)(2,1)}) custom-call(s32[768]{0:T(1024)} %reshape.62.src_ref, bf16[512,4096]{1,0:T(8,128)(2,1)} %x_ref.1), custom_call_target="tpu_custom_call" | custom-call | tf_op jit(solution)/shard_map/first_send/pallas_call | solution.py:58
  34.2 22.1 %all-gather.3.cloned.1.call-done.held_ref = bf16[3200,256]{1,0:T(8,128)(2,1)} async-done(((bf16[800,256]{1,0:T(8,128)(2,1)}), bf16[3200,256]{1,0:T(8,128)(2,1)}) %all-gather.3.cloned.1.call-update) | async-done | bytes 1638416 | tf_op jit(solution)/shard_map/all_gather | solution.py:201
  56.3 5.1 %next_send.1 = (bf16[8192,128]{1,0:T(8,128)(2,1)}, bf16[3200,256]{1,0:T(8,128)(2,1)}) custom-call(s32[256]{0:T(256)} %slice.33.src_ref, bf16[16384,128]{1,0:T(8,128)(2,1)} %get-tuple-element.10.y_ref, bf16[3200,256]{1,0:T(8,128)(2,1)} %all-gather.3.cloned.1.call-done.held_ref), custom_call_target="tpu_custom_call", output_to_operand_aliasing={{1}: (2, {})} | custom-call | tf_op jit(solution)/shard_map/next_send/pallas_call | solution.py:82
  61.6 22.0 %all_to_all.27 = s32[256,1,4]{2,1,0:T(1,128)S(1)} all-to-all(s32[256,1,4]{2,1,0:T(1,128)S(1)} %copy.13), channel_id=1, replica_groups=mesh['gx'=4,'zhi'=4,'core'=2,'gz'=8] {'gx','zhi','core','gz'}, dimensions={0} | all-to-all | bytes 8192 | tf_op jit(solution)/shard_map/all_to_all | solution.py:221
  83.6 150.7 %all_to_all.28 = bf16[256,96,128]{2,1,0:T(8,128)(2,1)} all-to-all(bf16[256,96,128]{2,1,0:T(8,128)(2,1)} %bitcast.20), channel_id=1, replica_groups=mesh['gx'=4,'zhi'=4,'core'=2,'gz'=8] {'gx','zhi','core','gz'}, dimensions={0} | all-to-all | bytes 12582912 | tf_op jit(solution)/shard_map/all_to_all | solution.py:234
  234.3 9.4 %all-to-all-start.1 = ((bf16[256,32,128]{2,1,0:T(8,128)(2,1)}), bf16[256,32,128]{2,1,0:T(8,128)(2,1)}, u32[]{:S(2)}, u32[]{:S(2)}) async-start(bf16[256,32,128]{2,1,0:T(8,128)(2,1)} %bitcast.21), calls=%async_computation.1 | async-start | bytes 4194304 | tf_op jit(solution)/shard_map/all_to_all | solution.py:234
  243.7 0.8 reshape.66.place_ref
  244.5 0.8 slice_reduce_fusion.place_ref
  245.2 35.9 %products.2.rest_0_ = f32[6656,256]{1,0:T(8,128)} custom-call(s32[768]{0:T(1024)} %reshape.66.place_ref, bf16[24576,128]{1,0:T(8,128)(2,1)} %bitcast.18, bf16[25600,256]{1,0:T(8,128)(2,1)} %all-gather.5.cloned.1.call-done.w_hbm), custom_call_target="tpu_custom_call" | custom-call | tf_op jit(solution)/shard_map/products/pallas_call | solution.py:166
  281.1 14.6 %all-to-all-done.1 = bf16[256,32,128]{2,1,0:T(8,128)(2,1)} async-done(((bf16[256,32,128]{2,1,0:T(8,128)(2,1)}), bf16[256,32,128]{2,1,0:T(8,128)(2,1)}, u32[]{:S(2)}, u32[]{:S(2)}) %all-to-all-start.1) | async-done | bytes 2097184 | tf_op jit(solution)/shard_map/all_to_all | solution.py:234
  295.7 19.5 %products.3 = bf16[6656,256]{1,0:T(8,128)(2,1)} custom-call(s32[256]{0:T(256)} %slice_reduce_fusion.place_ref, bf16[8192,128]{1,0:T(8,128)(2,1)} %bitcast.8.x_ref, bf16[25600,256]{1,0:T(8,128)(2,1)} %all-gather.5.cloned.1.call-done.w_hbm, f32[6656,256]{1,0:T(8,128)} %products.2.rest_0_), custom_call_target="tpu_custom_call" | custom-call | tf_op jit(solution)/shard_map/products/pallas_call | solution.py:166
  315.2 45.8 %all_to_all.29 = bf16[8,832,256]{2,1,0:T(8,128)(2,1)} all-to-all(bf16[8,832,256]{2,1,0:T(8,128)(2,1)} %bitcast.19), channel_id=1, replica_groups=mesh['gx'=4,'zhi'=4,'core'=2,'gz'=8] {'gz'}, dimensions={0} | all-to-all | bytes 6815744 | tf_op jit(solution)/shard_map/all_to_all | solution.py:241
  361.0 2.6 reduce_sum.42
  363.6 0.4 copy.15
  364.1 0.9 reshape.71
  (21 shorter events, 0.4 us)
Async XLA Ops:
  6.5 1.4 copy-start
  6.5 3.1 copy-start.1
  6.5 6.3 %copy-start.2 = (s32[3150]{0:T(1024)S(1)}, s32[3150]{0:T(1024)}, u32[]{:S(2)}) copy-start(s32[3150]{0:T(1024)} %param.10) | copy-start | bytes 37804
  6.5 49.7 %all-gather.3.cloned.1.call-start = ((), (), s32[]{:S(2)}) async-start(), calls=%async_computation.4 | async-start | bytes 2048000 | tf_op jit(solution)/shard_map/all_gather | solution.py:201
  8.8 236.5 %all-gather.5.cloned.1.call-start = ((), (), s32[]{:S(2)}) async-start(), calls=%async_computation.5 | async-start | bytes 14745600 | tf_op jit(solution)/shard_map/all_gather | solution.py:233
  234.3 61.5 %all-to-all-start.1 = ((bf16[256,32,128]{2,1,0:T(8,128)(2,1)}), bf16[256,32,128]{2,1,0:T(8,128)(2,1)}, u32[]{:S(2)}, u32[]{:S(2)}) async-start(bf16[256,32,128]{2,1,0:T(8,128)(2,1)} %bitcast.21), calls=%async_computation.1 | async-start | bytes 4194304 | tf_op jit(solution)/shard_map/all_to_all | solution.py:234
Sparse Core Ops, SparseCore 0:
  9.1 47.0 all-gather.2
  61.6 113.4 all-gather.4

commit v2 on v1

--- a/solution.py
+++ b/solution.py
@@ -23,9 +23,13 @@
     def _():
         def one(g, carry):
             v = x_ref[pl.ds(pl.multiple_of(g * 8, 8), 8), :].astype(jnp.float32)
+            half = lax.rem(g, 2)
             for q in range(q_rows):
-                tmp[pl.ds(q, 8, stride=q_rows), :] = v[:, q * 128:(q + 1) * 128]
-            y_ref[pl.ds(pl.multiple_of(g * span, span), span), :] = tmp[...].astype(y_ref.dtype)
+                tmp[half, pl.ds(q * 8, 8), :] = v[:, q * 128:(q + 1) * 128]
+            for r in range(8):
+                y_ref[pl.ds(pl.multiple_of(g * span, span) + r * q_rows, q_rows), :] = tmp[
+                    half, pl.ds(r, q_rows, stride=8), :
+                ].astype(y_ref.dtype)
             return carry
 
         lax.fori_loop(0, tiles // 8, one, 0, unroll=2)
@@ -65,7 +69,7 @@
                 pl.BlockSpec((block * q_rows, 128), lambda i, s: (i, 0)),
                 pl.BlockSpec((tiles * q_rows, 128), lambda i, s: (0, 0)),
             ],
-            scratch_shapes=[pltpu.VMEM((8 * q_rows, 128), jnp.float32)],
+            scratch_shapes=[pltpu.VMEM((2, 8 * q_rows, 128), jnp.float32)],
         ),
         out_shape=[
             jax.ShapeDtypeStruct((slots * q_rows, 128), x.dtype),
@@ -103,88 +107,108 @@
     )(src, y, held)
 
 
-def _product_kernel(has_in, last, unroll, place_ref, x_ref, w_hbm, *rest):
+def _product_kernel(has_in, last, block, unroll, place_ref, x_hbm, w_hbm, *rest):
     if has_in:
-        acc_in, out_ref, acc, wbuf, prod, sem = rest
+        acc_in, out_hbm, acc, w_ref, prod, xbuf, before, held, x_sem, sem = rest
     else:
-        out_ref, acc, wbuf, prod, sem = rest
-    step = pl.program_id(0)
-    edge = 64
-    out_rows = out_ref.shape[0]
-
-    @pl.when(step == 0)
-    def _():
-        copy = pltpu.make_async_copy(w_hbm, wbuf, sem.at[0])
-        copy.start()
-        if has_in:
-            back = pltpu.make_async_copy(acc_in, acc.at[pl.ds(0, out_rows), :], sem.at[1])
-            back.start()
-            back.wait()
-        else:
-            acc[...] = jnp.zeros_like(acc)
-        copy.wait()
-
-    block = x_ref.shape[0] // 32
-    base = step * block
-
-    def group(i, carry):
-        rows = []
-        for u in range(unroll):
-            n = i * unroll + u
-            v = place_ref[base + n]
-            row = lax.shift_right_logical(v, 10)
-            kc = lax.bitwise_and(v, 1023)
-            rows.append(row)
-            p = x_ref[pl.ds(pl.multiple_of(n * 32, 32), 32), :]
-            a = jnp.concatenate([p[:, :64], p[:, 64:]], axis=0)
-            w = jnp.concatenate(
-                [wbuf[pl.ds(pl.multiple_of((kc + 400 * k) * 16, 16), 16), :] for k in range(4)], axis=0
-            )
-            prod[u] = jnp.dot(a, w, preferred_element_type=jnp.float32)
-        for u in range(unroll):
-            where = pl.ds(pl.multiple_of(rows[u] * edge, edge), edge)
-            acc[where, :] += prod[u]
+        out_hbm, acc, w_ref, prod, xbuf, x_sem, sem = rest
+    rows = out_hbm.shape[0]
+    blocks = x_hbm.shape[0] // block
+
+    def fetch(b, slot):
+        return pltpu.make_async_copy(x_hbm.at[pl.ds(b * block, block)], xbuf.at[slot], x_sem.at[slot])
+
+    slab = pltpu.make_async_copy(w_hbm, w_ref, sem.at[0])
+    slab.start()
+    fetch(0, 0).start()
+    if has_in:
+        back = pltpu.make_async_copy(acc_in, before, sem.at[1])
+        back.start()
+    acc[...] = jnp.zeros_like(acc)
+    slab.wait()
+
+    def one_block(b, carry):
+        slot = lax.rem(b, 2)
+
+        @pl.when(b + 1 < blocks)
+        def _():
+            fetch(b + 1, 1 - slot).start()
+
+        fetch(b, slot).wait()
+
+        def group(i, carry):
+            where = []
+            for u in range(unroll):
+                n = i * unroll + u
+                v = place_ref[b * block + n]
+                where.append(lax.shift_right_logical(v, 10))
+                kc = lax.bitwise_and(v, 1023)
+                p = xbuf[slot, n]
+                a = jnp.concatenate([p[:, :64], p[:, 64:]], axis=0)
+                w = jnp.concatenate([w_ref[k, kc] for k in range(4)], axis=0)
+                prod[u] = jnp.dot(a, w, preferred_element_type=jnp.float32)
+            for u in range(unroll):
+                acc[where[u]] += prod[u]
+            return carry
+
+        lax.fori_loop(0, block // unroll, group, 0)
         return carry
 
-    lax.fori_loop(0, block // unroll, group, 0)
-
-    @pl.when(step == pl.num_programs(0) - 1)
-    def _():
-        if last:
-            out_ref[...] = acc[pl.ds(0, out_rows), :].astype(out_ref.dtype)
-        else:
-            away = pltpu.make_async_copy(acc.at[pl.ds(0, out_rows), :], out_ref, sem.at[1])
-            away.start()
-            away.wait()
-
-
-def products(place, x, w, acc_in, row_local, last, block=64, unroll=8):
-    tiles = place.shape[0]
+    lax.fori_loop(0, blocks, one_block, 0)
+    if has_in:
+        back.wait()
+    if last:
+        def finish(r, carry):
+            held[r] = (acc[r] + before[r]).astype(held.dtype) if has_in else acc[r].astype(held.dtype)
+            return carry
+
+        lax.fori_loop(0, rows, finish, 0, unroll=4)
+        away = pltpu.make_async_copy(held, out_hbm, sem.at[2])
+    else:
+        away = pltpu.make_async_copy(acc.at[pl.ds(0, rows)], out_hbm, sem.at[2])
+    away.start()
+    away.wait()
+
+
+def products(place, x, w, acc_in, row_local, last, block=128, unroll=8):
     has_in = acc_in is not None
-    rows = row_local * 64
     operands = (place, x, w) + ((acc_in,) if has_in else ())
+    edge, columns = 64, w.shape[-1]
+    result = jax.ShapeDtypeStruct((row_local, edge, columns), jnp.bfloat16 if last else jnp.float32)
     return pl.pallas_call(
-        functools.partial(_product_kernel, has_in, last, unroll),
-        grid_spec=pltpu.PrefetchScalarGridSpec(
-            num_scalar_prefetch=1,
-            grid=(tiles // block,),
-            in_specs=[
-                pl.BlockSpec((block * 32, 128), lambda i, s: (i, 0)),
-                pl.BlockSpec(memory_space=pl.ANY),
-            ] + ([pl.BlockSpec(memory_space=pl.ANY)] if has_in else []),
-            out_specs=pl.BlockSpec((rows, 256), lambda i, s: (0, 0)) if last
-            else pl.BlockSpec(memory_space=pl.ANY),
-            scratch_shapes=[
-                pltpu.VMEM((rows + 64, 256), jnp.float32),
-                pltpu.VMEM(w.shape, w.dtype),
-                pltpu.VMEM((unroll, 64, 256), jnp.float32),
-                pltpu.SemaphoreType.DMA((2,)),
-            ],
-        ),
-        out_shape=jax.ShapeDtypeStruct((rows, 256), jnp.bfloat16 if last else jnp.float32),
+        functools.partial(_product_kernel, has_in, last, block, unroll),
+        in_specs=[pl.BlockSpec(memory_space=pltpu.SMEM)] + [pl.BlockSpec(memory_space=pl.ANY)] * (len(operands) - 1),
+        out_specs=pl.BlockSpec(memory_space=pl.ANY),
+        scratch_shapes=[
+            pltpu.VMEM((row_local + 1, edge, columns), jnp.float32),
+            pltpu.VMEM(w.shape, w.dtype),
+            pltpu.VMEM((unroll, edge, columns), jnp.float32),
+            pltpu.VMEM((2, block, 32, 128), x.dtype),
+        ] + ([
+            pltpu.VMEM((row_local, edge, columns), jnp.float32),
+            pltpu.VMEM(result.shape, result.dtype),
+        ] if has_in else []) + [
+            pltpu.SemaphoreType.DMA((2,)),
+            pltpu.SemaphoreType.DMA((3,)),
+        ],
+        out_shape=result,
         compiler_params=pltpu.CompilerParams(vmem_limit_bytes=VMEM_LIMIT),
         name="products",
     )(*operands)
+
+
+def look_up(coords, row_slot, kc_slot):
+    count = row_slot.shape[0]
+    lines = -(-count // 128)
+    tables = jnp.pad(jnp.stack([row_slot, kc_slot]), ((0, 0), (0, lines * 128 - count)))
+    tables = tables.reshape(2, lines, 128).astype(jnp.float32)
+    line = (coords[:, :, None] // 128 == jnp.arange(lines)).astype(jnp.float32)
+    picked = jnp.einsum(
+        "tnh,thl->tnl", line, tables, precision=lax.Precision.HIGHEST, preferred_element_type=jnp.float32
+    )
+    lane = coords[:, :, None] % 128 == jnp.arange(128)
+    found = jnp.sum(jnp.where(lane, picked, 0.0), axis=2).astype(jnp.int32)
+    return found[0], found[1]
 
 
 def body(amplitudes, tile_coords, row_slot, kc_slot, integrals):
@@ -200,8 +224,7 @@
     quarter = quarter.reshape(kc_piece * part, columns)
     slab = lax.all_gather(quarter, "zhi", axis=0, tiled=True)
 
-    row_pos = jnp.take(row_slot, tile_coords[:, 0])
-    kc_pos = jnp.take(kc_slot, tile_coords[:, 1])
+    row_pos, kc_pos = look_up(tile_coords.T, row_slot, kc_slot)
     kc_target = kc_pos // kc_piece % kc_groups
     kc_gy = kc_pos // (kc_groups * kc_piece)
     kc_row = kc_gy % 2 * (kc_piece * gy_size // 2) + kc_gy // 2 * kc_piece + kc_pos % kc_piece
@@ -231,13 +254,11 @@
         else:
             sent, slab = next_send(src, relaid, slab, 64)
             slab = lax.all_gather(slab, ("gx", "core"), axis=0, tiled=True)
-        arrived = lax.all_to_all(
-            sent.reshape(devices, size * 32, 128), ALL, split_axis=0, concat_axis=0, tiled=True
-        )
-        got.append((arrived.reshape(devices * size * 32, 128), got_place[:, start:start + size].reshape(-1)))
+        arrived = lax.all_to_all(sent.reshape(devices, size * 32, 128), ALL, split_axis=0, concat_axis=0, tiled=True)
+        got.append((arrived.reshape(devices * size, 32, 128), got_place[:, start:start + size].reshape(-1)))
         start += size
     for index, (tiles, places) in enumerate(got):
-        acc = products(places, tiles, slab, acc, row_local, index == len(got) - 1)
+        acc = products(places, tiles, slab.reshape(planes, -1, part, columns), acc, row_local, index == len(got) - 1)
     shared = lax.all_to_all(
         acc.reshape(kc_groups, row_local // kc_groups * tile_edge, columns), "gz", split_axis=0, concat_axis=0, tiled=True
     )
@@ -257,6 +278,4 @@
         P(GY + ("gz",), None, None),
     )
 
-    return jax.shard_map(
-        body, mesh=fine, in_specs=placed, out_specs=P(ALL, None, None), check_vma=False
-    )
+    return jax.shard_map(body, mesh=fine, in_specs=placed, out_specs=P(ALL, None, None), check_vma=False)

time: 374 us -> 371 us (level)
  waiting for transfers between devices: 36.8 us -> 45.6 us
  Pallas kernels: 76.2 us -> 69 us
  local copies, waits for them, and re-layouts: 13.9 us -> 8.3 us
    all_gather x1, waiting for transfers between devices: 22.1 us -> 29.5 us  [body(): slab = lax.all_gather(quarter, 'zhi', axis=0, tiled=True)]
    gather x2 -> x0, local copies, waits for them, and re-layouts: 6.29 us -> none  [the longest x1 3.14 us: body(): row_pos = jnp.take(row_slot, tile_coords[:, 0])]
    pallas_call x2, Pallas kernels: 55.3 us -> 51.3 us  [products(): pl.pallas_call(functools.partial(_product_kernel, has_in, last, block, un...]
  transfers between devices with their start and end apart: 3 -> 3, of which waited for: 2 -> 2; matrix products, arithmetic and copies ran while one was open for 3% -> 2% of each run, Pallas kernels for 14% -> 13%
where the time goes in v2:
time: 371 us; the launch traced here: 369 us
  blocking collectives  218 us (59%)
  Pallas kernels  69 us (19%)
  waiting for transfers between devices  45.6 us (12%)
  between operations  13.5 us (4%)
  starting transfers between devices  9.42 us (3%)
  local copies, waits for them, and re-layouts  8.3 us (2%)
  other arithmetic  4.5 us (1%)
    all_to_all x1, blocking collectives, body(): lax.all_to_all(sent.reshape(devices, size * 32, 128), ALL, split_axis=0,...  151 us
    pallas_call x2, Pallas kernels, products(): pl.pallas_call(functools.partial(_product_kernel, has_in, last, block, un...  51.3 us
    all_to_all x1, blocking collectives, body(): lax.all_to_all(acc.reshape(kc_groups, row_local // kc_groups * tile_edge,...  45.8 us
    all_gather x1, waiting for transfers between devices, body(): slab = lax.all_gather(quarter, 'zhi', axis=0, tiled=True)  29.5 us
    all_to_all x1, blocking collectives, body(): lax.all_to_all(sent_place, ALL, split_axis=0, concat_axis=0, tiled=True)  22.1 us
    all_to_all x1, waiting for transfers between devices, body(): lax.all_to_all(sent.reshape(devices, size * 32, 128), ALL, split_axis=0,...  16.1 us
    pallas_call x1, Pallas kernels, first_send(): pl.pallas_call(_relayout_kernel, grid_spec=pltpu.PrefetchScalarGridSpec(n...  12.6 us
    all_to_all x1, starting transfers between devices, body(): lax.all_to_all(sent.reshape(devices, size * 32, 128), ALL, split_axis=0,...  9.37 us
  transfers between devices with their start and end apart: 3, of which 2 were waited for; matrix products, arithmetic and copies ran while one was open for 2% of the time, Pallas kernels for 13%

profile of v2, /device:TPU:2, one launch (start us, length us, event | category | flops | bytes accessed | tf_op | source)
XLA Modules:
  0.0 369.3 jit_solution(6868498806904609462)
XLA Ops:
  6.5 1.4 copy-done
  8.0 0.8 constant_dynamic-slice_fusion
  8.8 0.7 stack.9
  9.6 0.7 stack.10
  10.4 0.7 and_select_fusion.6
  11.1 0.5 fusion
  12.0 0.7 select_reduce_fusion
  12.7 0.6 slice.33.src_ref
  13.4 0.8 reshape.160.src_ref
  14.3 12.6 %first_send.1 = (bf16[24576,128]{1,0:T(8,128)(2,1)}, bf16[16384,128]{1,0:T(8,128)(2,1)}) custom-call(s32[768]{0:T(1024)} %reshape.160.src_ref, bf16[512,4096]{1,0:T(8,128)(2,1)} %x_ref.1), custom_call_target="tpu_custom_call" | custom-call | tf_op jit(solution)/shard_map/first_send/pallas_call | solution.py:62
  26.8 29.5 %all-gather.3.cloned.1.call-done.held_ref = bf16[3200,256]{1,0:T(8,128)(2,1)} async-done(((bf16[800,256]{1,0:T(8,128)(2,1)}), bf16[3200,256]{1,0:T(8,128)(2,1)}) %all-gather.3.cloned.1.call-update) | async-done | bytes 1638416 | tf_op jit(solution)/shard_map/all_gather | solution.py:225
  56.3 5.1 %next_send.1 = (bf16[8192,128]{1,0:T(8,128)(2,1)}, bf16[3200,256]{1,0:T(8,128)(2,1)}) custom-call(s32[256]{0:T(256)} %slice.33.src_ref, bf16[16384,128]{1,0:T(8,128)(2,1)} %get-tuple-element.9.y_ref, bf16[3200,256]{1,0:T(8,128)(2,1)} %all-gather.3.cloned.1.call-done.held_ref), custom_call_target="tpu_custom_call", output_to_operand_aliasing={{1}: (2, {})} | custom-call | tf_op jit(solution)/shard_map/next_send/pallas_call | solution.py:86
  61.6 22.1 %all_to_all.27 = s32[256,1,4]{2,1,0:T(1,128)S(1)} all-to-all(s32[256,1,4]{2,1,0:T(1,128)S(1)} %copy.13), channel_id=1, replica_groups=mesh['gx'=4,'zhi'=4,'core'=2,'gz'=8] {'gx','zhi','core','gz'}, dimensions={0} | all-to-all | bytes 8192 | tf_op jit(solution)/shard_map/all_to_all | solution.py:244
  83.7 150.7 %all_to_all.28 = bf16[256,96,128]{2,1,0:T(8,128)(2,1)} all-to-all(bf16[256,96,128]{2,1,0:T(8,128)(2,1)} %bitcast.47), channel_id=1, replica_groups=mesh['gx'=4,'zhi'=4,'core'=2,'gz'=8] {'gx','zhi','core','gz'}, dimensions={0} | all-to-all | bytes 12582912 | tf_op jit(solution)/shard_map/all_to_all | solution.py:257
  234.3 9.4 %all-to-all-start.1 = ((bf16[256,32,128]{2,1,0:T(8,128)(2,1)}), bf16[256,32,128]{2,1,0:T(8,128)(2,1)}, u32[]{:S(2)}, u32[]{:S(2)}) async-start(bf16[256,32,128]{2,1,0:T(8,128)(2,1)} %bitcast.48), calls=%async_computation.1 | async-start | bytes 4194304 | tf_op jit(solution)/shard_map/all_to_all | solution.py:257
  243.7 0.8 reshape.164.place_ref
  244.5 0.8 slice_reduce_fusion.place_ref
  245.3 34.4 %products.2.rest_0_ = f32[104,64,256]{2,1,0:T(8,128)} custom-call(s32[768]{0:T(1024)} %reshape.164.place_ref, bf16[768,32,128]{2,1,0:T(8,128)(2,1)} %bitcast.45, bf16[4,400,16,256]{3,2,1,0:T(8,128)(2,1)} %bitcast.43), custom_call_target="tpu_custom_call" | custom-call | tf_op jit(solution)/shard_map/products/pallas_call | solution.py:178
  279.7 16.1 %all-to-all-done.1.x_hbm = bf16[256,32,128]{2,1,0:T(8,128)(2,1)} async-done(((bf16[256,32,128]{2,1,0:T(8,128)(2,1)}), bf16[256,32,128]{2,1,0:T(8,128)(2,1)}, u32[]{:S(2)}, u32[]{:S(2)}) %all-to-all-start.1) | async-done | bytes 2097184 | tf_op jit(solution)/shard_map/all_to_all | solution.py:257
  295.8 16.9 %products.3 = bf16[104,64,256]{2,1,0:T(8,128)(2,1)} custom-call(s32[256]{0:T(256)} %slice_reduce_fusion.place_ref, bf16[256,32,128]{2,1,0:T(8,128)(2,1)} %all-to-all-done.1.x_hbm, bf16[4,400,16,256]{3,2,1,0:T(8,128)(2,1)} %bitcast.44, f32[104,64,256]{2,1,0:T(8,128)} %products.2.rest_0_), custom_call_target="tpu_custom_call" | custom-call | tf_op jit(solution)/shard_map/products/pallas_call | solution.py:178
  312.7 45.8 %all_to_all.29 = bf16[8,832,256]{2,1,0:T(8,128)(2,1)} all-to-all(bf16[8,832,256]{2,1,0:T(8,128)(2,1)} %bitcast.46), channel_id=1, replica_groups=mesh['gx'=4,'zhi'=4,'core'=2,'gz'=8] {'gz'}, dimensions={0} | all-to-all | bytes 6815744 | tf_op jit(solution)/shard_map/all_to_all | solution.py:262
  358.5 2.6 reduce_sum.52
  361.1 0.4 copy.15
  361.5 0.9 reshape.169
  (21 shorter events, 0.8 us)
Async XLA Ops:
  6.5 1.4 copy-start
  6.5 49.8 %all-gather.3.cloned.1.call-start = ((), (), s32[]{:S(2)}) async-start(), calls=%async_computation.4 | async-start | bytes 2048000 | tf_op jit(solution)/shard_map/all_gather | solution.py:225
  8.8 236.5 %all-gather.5.cloned.1.call-start = ((), (), s32[]{:S(2)}) async-start(), calls=%async_computation.5 | async-start | bytes 14745600 | tf_op jit(solution)/shard_map/all_gather | solution.py:256
  234.3 61.5 %all-to-all-start.1 = ((bf16[256,32,128]{2,1,0:T(8,128)(2,1)}), bf16[256,32,128]{2,1,0:T(8,128)(2,1)}, u32[]{:S(2)}, u32[]{:S(2)}) async-start(bf16[256,32,128]{2,1,0:T(8,128)(2,1)} %bitcast.48), calls=%async_computation.1 | async-start | bytes 4194304 | tf_op jit(solution)/shard_map/all_to_all | solution.py:257
Sparse Core Ops, SparseCore 0:
  9.1 47.1 all-gather.2
  61.6 113.4 all-gather.4

commit v3 on v2

--- a/solution.py
+++ b/solution.py
@@ -10,49 +10,48 @@
 ALL = ("gx", "zhi", "core", "gz")
 GY = ("zhi", "core")
 CAP = 4
+RELAYOUT = 4
 CHUNKS = (3, 1)
 VMEM_LIMIT = 62 * 1024 * 1024
 
 
-def _relayout_kernel(src_ref, x_ref, out_ref, y_ref, tmp):
+def _relayout_kernel(src_ref, x_ref, out_ref, y_ref, *tmps):
     tiles = x_ref.shape[0]
     q_rows = x_ref.shape[1] // 128
-    span = 8 * q_rows
+    group = 8 * len(tmps)
 
     @pl.when(pl.program_id(0) == 0)
     def _():
         def one(g, carry):
-            v = x_ref[pl.ds(pl.multiple_of(g * 8, 8), 8), :].astype(jnp.float32)
-            half = lax.rem(g, 2)
-            for q in range(q_rows):
-                tmp[half, pl.ds(q * 8, 8), :] = v[:, q * 128:(q + 1) * 128]
-            for r in range(8):
-                y_ref[pl.ds(pl.multiple_of(g * span, span) + r * q_rows, q_rows), :] = tmp[
-                    half, pl.ds(r, q_rows, stride=8), :
-                ].astype(y_ref.dtype)
+            for t, tmp in enumerate(tmps):
+                v = x_ref[pl.ds(pl.multiple_of(g * group, group) + 8 * t, 8), :].astype(jnp.float32)
+                for q in range(q_rows):
+                    tmp[pl.ds(q * 8, 8), :] = v[:, q * 128:(q + 1) * 128]
+            for t, tmp in enumerate(tmps):
+                for r in range(8):
+                    y_ref[g * group + 8 * t + r] = tmp[pl.ds(r, q_rows, stride=8), :].astype(y_ref.dtype)
             return carry
 
-        lax.fori_loop(0, tiles // 8, one, 0, unroll=2)
-
-    _copy_slots(src_ref, y_ref, out_ref, q_rows)
-
-
-def _copy_slots(src_ref, y_ref, out_ref, q_rows):
-    slots = out_ref.shape[0] // q_rows
+        lax.fori_loop(0, tiles // group, one, 0)
+
+    _copy_slots(src_ref, y_ref, out_ref)
+
+
+def _copy_slots(src_ref, y_ref, out_ref):
+    slots = out_ref.shape[0]
     base = pl.program_id(0) * slots
 
-    def one(s, carry):
-        n = src_ref[base + s]
-        out_ref[pl.ds(pl.multiple_of(s * q_rows, q_rows), q_rows), :] = y_ref[
-            pl.ds(pl.multiple_of(n * q_rows, q_rows), q_rows), :
-        ]
+    def one(g, carry):
+        for u in range(16):
+            s = g * 16 + u
+            out_ref[s] = y_ref[src_ref[base + s]]
         return carry
 
-    lax.fori_loop(0, slots, one, 0, unroll=16)
+    lax.fori_loop(0, slots // 16, one, 0)
 
 
 def _copy_kernel(src_ref, y_ref, held_ref, out_ref, kept_ref):
-    _copy_slots(src_ref, y_ref, out_ref, 32)
+    _copy_slots(src_ref, y_ref, out_ref)
 
 
 def first_send(src, x, block):
@@ -66,14 +65,14 @@
             grid=(slots // block,),
             in_specs=[pl.BlockSpec((tiles, width), lambda i, s: (0, 0))],
             out_specs=[
-                pl.BlockSpec((block * q_rows, 128), lambda i, s: (i, 0)),
-                pl.BlockSpec((tiles * q_rows, 128), lambda i, s: (0, 0)),
+                pl.BlockSpec((block, q_rows, 128), lambda i, s: (i, 0, 0)),
+                pl.BlockSpec((tiles, q_rows, 128), lambda i, s: (0, 0, 0)),
             ],
-            scratch_shapes=[pltpu.VMEM((2, 8 * q_rows, 128), jnp.float32)],
+            scratch_shapes=[pltpu.VMEM((8 * q_rows, 128), jnp.float32) for _ in range(RELAYOUT)],
         ),
         out_shape=[
-            jax.ShapeDtypeStruct((slots * q_rows, 128), x.dtype),
-            jax.ShapeDtypeStruct((tiles * q_rows, 128), x.dtype),
+            jax.ShapeDtypeStruct((slots, q_rows, 128), x.dtype),
+            jax.ShapeDtypeStruct((tiles, q_rows, 128), x.dtype),
         ],
         compiler_params=pltpu.CompilerParams(vmem_limit_bytes=VMEM_LIMIT),
         name="first_send",
@@ -81,7 +80,6 @@
 
 
 def next_send(src, y, held, block):
-    rows = y.shape[0]
     slots = src.shape[0]
     return pl.pallas_call(
         _copy_kernel,
@@ -89,16 +87,16 @@
             num_scalar_prefetch=1,
             grid=(slots // block,),
             in_specs=[
-                pl.BlockSpec((rows, 128), lambda i, s: (0, 0)),
+                pl.BlockSpec(y.shape, lambda i, s: (0, 0, 0)),
                 pl.BlockSpec(memory_space=pl.ANY),
             ],
             out_specs=[
-                pl.BlockSpec((block * 32, 128), lambda i, s: (i, 0)),
+                pl.BlockSpec((block,) + y.shape[1:], lambda i, s: (i, 0, 0)),
                 pl.BlockSpec(memory_space=pl.ANY),
             ],
         ),
         out_shape=[
-            jax.ShapeDtypeStruct((slots * 32, 128), y.dtype),
+            jax.ShapeDtypeStruct((slots,) + y.shape[1:], y.dtype),
             jax.ShapeDtypeStruct(held.shape, held.dtype),
         ],
         input_output_aliases={2: 1},
@@ -170,7 +168,7 @@
     away.wait()
 
 
-def products(place, x, w, acc_in, row_local, last, block=128, unroll=8):
+def products(place, x, w, acc_in, row_local, last, block=128, unroll=32):
     has_in = acc_in is not None
     operands = (place, x, w) + ((acc_in,) if has_in else ())
     edge, columns = 64, w.shape[-1]

time: 371 us -> 367 us (0.989)
  Pallas kernels: 69 us -> 49.4 us
  waiting for transfers between devices: 45.6 us -> 60.6 us
    pallas_call x2, Pallas kernels: 51.3 us -> 32.9 us  [products(): pl.pallas_call(functools.partial(_product_kernel, has_in, last, block, un...]
    all_to_all x1, waiting for transfers between devices: 16.1 us -> 30.2 us  [body(): lax.all_to_all(sent.reshape(devices, size * 32, 128), ALL, split_axis=0,...]
  transfers between devices with their start and end apart: 3 -> 3, of which waited for: 2 -> 2; matrix products, arithmetic and copies ran while one was open for 2% -> 2% of each run, Pallas kernels for 13% -> 9%
where the time goes in v3:
time: 367 us; the launch traced here: 365 us
  blocking collectives  218 us (59%)
  waiting for transfers between devices  60.6 us (17%)
  Pallas kernels  49.4 us (13%)
  between operations  13.5 us (4%)
  starting transfers between devices  9.42 us (3%)
  local copies, waits for them, and re-layouts  8.3 us (2%)
  other arithmetic  4.5 us (1%)
    all_to_all x1, blocking collectives, body(): lax.all_to_all(sent.reshape(devices, size * 32, 128), ALL, split_axis=0,...  151 us
    all_to_all x1, blocking collectives, body(): lax.all_to_all(acc.reshape(kc_groups, row_local // kc_groups * tile_edge,...  45.8 us
    pallas_call x2, Pallas kernels, products(): pl.pallas_call(functools.partial(_product_kernel, has_in, last, block, un...  32.9 us
    all_gather x1, waiting for transfers between devices, body(): slab = lax.all_gather(quarter, 'zhi', axis=0, tiled=True)  30.4 us
    all_to_all x1, waiting for transfers between devices, body(): lax.all_to_all(sent.reshape(devices, size * 32, 128), ALL, split_axis=0,...  30.2 us
    all_to_all x1, blocking collectives, body(): lax.all_to_all(sent_place, ALL, split_axis=0, concat_axis=0, tiled=True)  22 us
    pallas_call x1, Pallas kernels, first_send(): pl.pallas_call(_relayout_kernel, grid_spec=pltpu.PrefetchScalarGridSpec(n...  11.6 us
    all_to_all x1, starting transfers between devices, body(): lax.all_to_all(sent.reshape(devices, size * 32, 128), ALL, split_axis=0,...  9.37 us
  transfers between devices with their start and end apart: 3, of which 2 were waited for; matrix products, arithmetic and copies ran while one was open for 2% of the time, Pallas kernels for 9%

profile of v3, /device:TPU:2, one launch (start us, length us, event | category | flops | bytes accessed | tf_op | source)
XLA Modules:
  0.0 364.7 jit_solution(7239635743612986830)
XLA Ops:
  6.5 1.4 copy-done
  8.0 0.8 constant_dynamic-slice_fusion
  8.8 0.7 stack.9
  9.6 0.7 stack.10
  10.4 0.7 and_select_fusion.6
  11.1 0.5 fusion
  12.0 0.7 select_reduce_fusion
  12.7 0.6 slice.33.src_ref
  13.4 0.8 reshape.157.src_ref
  14.3 11.6 %first_send.1 = (bf16[768,32,128]{2,1,0:T(8,128)(2,1)}, bf16[512,32,128]{2,1,0:T(8,128)(2,1)}) custom-call(s32[768]{0:T(1024)} %reshape.157.src_ref, bf16[512,4096]{1,0:T(8,128)(2,1)} %x_ref.1), custom_call_target="tpu_custom_call" | custom-call | tf_op jit(solution)/shard_map/first_send/pallas_call | solution.py:61
  25.9 30.4 %all-gather.3.cloned.1.call-done.held_ref = bf16[3200,256]{1,0:T(8,128)(2,1)} async-done(((bf16[800,256]{1,0:T(8,128)(2,1)}), bf16[3200,256]{1,0:T(8,128)(2,1)}) %all-gather.3.cloned.1.call-update) | async-done | bytes 1638416 | tf_op jit(solution)/shard_map/all_gather | solution.py:223
  56.3 4.9 %next_send.1 = (bf16[256,32,128]{2,1,0:T(8,128)(2,1)}, bf16[3200,256]{1,0:T(8,128)(2,1)}) custom-call(s32[256]{0:T(256)} %slice.33.src_ref, bf16[512,32,128]{2,1,0:T(8,128)(2,1)} %get-tuple-element.9.y_ref, bf16[3200,256]{1,0:T(8,128)(2,1)} %all-gather.3.cloned.1.call-done.held_ref), custom_call_target="tpu_custom_call", output_to_operand_aliasing={{1}: (2, {})} | custom-call | tf_op jit(solution)/shard_map/next_send/pallas_call | solution.py:84
  61.3 22.0 %all_to_all.27 = s32[256,1,4]{2,1,0:T(1,128)S(1)} all-to-all(s32[256,1,4]{2,1,0:T(1,128)S(1)} %copy.13), channel_id=1, replica_groups=mesh['gx'=4,'zhi'=4,'core'=2,'gz'=8] {'gx','zhi','core','gz'}, dimensions={0} | all-to-all | bytes 8192 | tf_op jit(solution)/shard_map/all_to_all | solution.py:242
  83.4 150.7 %all_to_all.28 = bf16[256,96,128]{2,1,0:T(8,128)(2,1)} all-to-all(bf16[256,96,128]{2,1,0:T(8,128)(2,1)} %bitcast.46), channel_id=1, replica_groups=mesh['gx'=4,'zhi'=4,'core'=2,'gz'=8] {'gx','zhi','core','gz'}, dimensions={0} | all-to-all | bytes 12582912 | tf_op jit(solution)/shard_map/all_to_all | solution.py:255
  234.0 9.4 %all-to-all-start.1 = ((bf16[256,32,128]{2,1,0:T(8,128)(2,1)}), bf16[256,32,128]{2,1,0:T(8,128)(2,1)}, u32[]{:S(2)}, u32[]{:S(2)}) async-start(bf16[256,32,128]{2,1,0:T(8,128)(2,1)} %get-tuple-element.10), calls=%async_computation.1 | async-start | bytes 4194304 | tf_op jit(solution)/shard_map/all_to_all | solution.py:255
  243.4 0.8 reshape.160.place_ref
  244.2 0.8 slice_reduce_fusion.place_ref
  245.0 20.4 %products.2.rest_0_ = f32[104,64,256]{2,1,0:T(8,128)} custom-call(s32[768]{0:T(1024)} %reshape.160.place_ref, bf16[768,32,128]{2,1,0:T(8,128)(2,1)} %bitcast.44, bf16[4,400,16,256]{3,2,1,0:T(8,128)(2,1)} %bitcast.42), custom_call_target="tpu_custom_call" | custom-call | tf_op jit(solution)/shard_map/products/pallas_call | solution.py:176
  265.3 30.2 %all-to-all-done.1.x_hbm = bf16[256,32,128]{2,1,0:T(8,128)(2,1)} async-done(((bf16[256,32,128]{2,1,0:T(8,128)(2,1)}), bf16[256,32,128]{2,1,0:T(8,128)(2,1)}, u32[]{:S(2)}, u32[]{:S(2)}) %all-to-all-start.1) | async-done | bytes 2097184 | tf_op jit(solution)/shard_map/all_to_all | solution.py:255
  295.5 12.6 %products.3 = bf16[104,64,256]{2,1,0:T(8,128)(2,1)} custom-call(s32[256]{0:T(256)} %slice_reduce_fusion.place_ref, bf16[256,32,128]{2,1,0:T(8,128)(2,1)} %all-to-all-done.1.x_hbm, bf16[4,400,16,256]{3,2,1,0:T(8,128)(2,1)} %bitcast.43, f32[104,64,256]{2,1,0:T(8,128)} %products.2.rest_0_), custom_call_target="tpu_custom_call" | custom-call | tf_op jit(solution)/shard_map/products/pallas_call | solution.py:176
  308.0 45.8 %all_to_all.29 = bf16[8,832,256]{2,1,0:T(8,128)(2,1)} all-to-all(bf16[8,832,256]{2,1,0:T(8,128)(2,1)} %bitcast.45), channel_id=1, replica_groups=mesh['gx'=4,'zhi'=4,'core'=2,'gz'=8] {'gz'}, dimensions={0} | all-to-all | bytes 6815744 | tf_op jit(solution)/shard_map/all_to_all | solution.py:260
  353.8 2.6 reduce_sum.52
  356.5 0.4 copy.15
  356.9 0.9 reshape.165
  (21 shorter events, 0.8 us)
Async XLA Ops:
  6.5 1.4 copy-start
  6.5 49.7 %all-gather.3.cloned.1.call-start = ((), (), s32[]{:S(2)}) async-start(), calls=%async_computation.4 | async-start | bytes 2048000 | tf_op jit(solution)/shard_map/all_gather | solution.py:223
  8.8 236.2 %all-gather.5.cloned.1.call-start = ((), (), s32[]{:S(2)}) async-start(), calls=%async_computation.5 | async-start | bytes 14745600 | tf_op jit(solution)/shard_map/all_gather | solution.py:254
  234.0 61.5 %all-to-all-start.1 = ((bf16[256,32,128]{2,1,0:T(8,128)(2,1)}), bf16[256,32,128]{2,1,0:T(8,128)(2,1)}, u32[]{:S(2)}, u32[]{:S(2)}) async-start(bf16[256,32,128]{2,1,0:T(8,128)(2,1)} %get-tuple-element.10), calls=%async_computation.1 | async-start | bytes 4194304 | tf_op jit(solution)/shard_map/all_to_all | solution.py:255
Sparse Core Ops, SparseCore 0:
  9.1 47.0 all-gather.2
  61.3 113.4 all-gather.4

commit v4 on v3

--- a/solution.py
+++ b/solution.py
@@ -105,25 +105,52 @@
     )(src, y, held)
 
 
-def _product_kernel(has_in, last, block, unroll, place_ref, x_hbm, w_hbm, *rest):
+def _held_kernel(*refs):
+    pass
+
+
+def held_until(values):
+    count = len(values)
+    return list(pl.pallas_call(
+        _held_kernel,
+        in_specs=[pl.BlockSpec(memory_space=pl.ANY)] * count,
+        out_specs=[pl.BlockSpec(memory_space=pl.ANY)] * count,
+        out_shape=[jax.ShapeDtypeStruct(v.shape, v.dtype) for v in values],
+        input_output_aliases={i: i for i in range(count)},
+        name="held_until",
+    )(*values))
+
+
+def _product_kernel(has_in, last, block, unroll, place_ref, own_ref, x_hbm, *rest):
+    parts, rest = rest[:8], rest[8:]
     if has_in:
-        acc_in, out_hbm, acc, w_ref, prod, xbuf, before, held, x_sem, sem = rest
+        acc_in, out_hbm, acc, w_ref, prod, xbuf, before, held, w_sem, x_sem, sem = rest
     else:
-        out_hbm, acc, w_ref, prod, xbuf, x_sem, sem = rest
+        out_hbm, acc, w_ref, prod, xbuf, w_sem, x_sem, sem = rest
     rows = out_hbm.shape[0]
     blocks = x_hbm.shape[0] // block
 
     def fetch(b, slot):
         return pltpu.make_async_copy(x_hbm.at[pl.ds(b * block, block)], xbuf.at[slot], x_sem.at[slot])
 
-    slab = pltpu.make_async_copy(w_hbm, w_ref, sem.at[0])
-    slab.start()
+    copies = []
+    for index, part in enumerate(parts):
+        plane = lax.rem(own_ref[0] + 4 - index % 4, 4)
+        core = lax.rem(own_ref[2] + index // 4, 2)
+        for back_z in range(4):
+            first = (core * 4 + lax.rem(own_ref[1] + 4 - back_z, 4)) * 50
+            copies.append(pltpu.make_async_copy(
+                part.at[back_z], w_ref.at[plane, pl.ds(first, 50)], w_sem.at[index * 4 + back_z]
+            ))
+    for copy in copies:
+        copy.start()
     fetch(0, 0).start()
     if has_in:
         back = pltpu.make_async_copy(acc_in, before, sem.at[1])
         back.start()
     acc[...] = jnp.zeros_like(acc)
-    slab.wait()
+    for copy in copies:
+        copy.wait()
 
     def one_block(b, carry):
         slot = lax.rem(b, 2)
@@ -168,24 +195,26 @@
     away.wait()
 
 
-def products(place, x, w, acc_in, row_local, last, block=128, unroll=32):
+def products(place, x, parts, own, acc_in, row_local, last, block=128, unroll=32):
     has_in = acc_in is not None
-    operands = (place, x, w) + ((acc_in,) if has_in else ())
-    edge, columns = 64, w.shape[-1]
+    operands = (place, own, x, *parts) + ((acc_in,) if has_in else ())
+    group, piece, rows, columns = parts[0].shape
+    edge = rows * group
     result = jax.ShapeDtypeStruct((row_local, edge, columns), jnp.bfloat16 if last else jnp.float32)
     return pl.pallas_call(
         functools.partial(_product_kernel, has_in, last, block, unroll),
-        in_specs=[pl.BlockSpec(memory_space=pltpu.SMEM)] + [pl.BlockSpec(memory_space=pl.ANY)] * (len(operands) - 1),
+        in_specs=[pl.BlockSpec(memory_space=pltpu.SMEM)] * 2 + [pl.BlockSpec(memory_space=pl.ANY)] * (len(operands) - 2),
         out_specs=pl.BlockSpec(memory_space=pl.ANY),
         scratch_shapes=[
             pltpu.VMEM((row_local + 1, edge, columns), jnp.float32),
-            pltpu.VMEM(w.shape, w.dtype),
+            pltpu.VMEM((4, 2 * group * piece, rows, columns), x.dtype),
             pltpu.VMEM((unroll, edge, columns), jnp.float32),
             pltpu.VMEM((2, block, 32, 128), x.dtype),
         ] + ([
             pltpu.VMEM((row_local, edge, columns), jnp.float32),
             pltpu.VMEM(result.shape, result.dtype),
         ] if has_in else []) + [
+            pltpu.SemaphoreType.DMA((32,)),
             pltpu.SemaphoreType.DMA((2,)),
             pltpu.SemaphoreType.DMA((3,)),
         ],
@@ -193,6 +222,11 @@
         compiler_params=pltpu.CompilerParams(vmem_limit_bytes=VMEM_LIMIT),
         name="products",
     )(*operands)
+
+
+def shifted(value, axis):
+    size = lax.axis_size(axis)
+    return [lax.ppermute(value, axis, [(d, (d + s) % size) for d in range(size)]) for s in range(1, size)]
 
 
 def look_up(coords, row_slot, kc_slot):
@@ -220,7 +254,8 @@
     part = tile_edge // planes
     quarter = lax.dynamic_slice_in_dim(integrals, lax.axis_index("gx") * part, part, 1)
     quarter = quarter.reshape(kc_piece * part, columns)
-    slab = lax.all_gather(quarter, "zhi", axis=0, tiled=True)
+    pieces = [quarter] + shifted(quarter, "zhi")
+    slab = jnp.concatenate(pieces, axis=0)
 
     row_pos, kc_pos = look_up(tile_coords.T, row_slot, kc_slot)
     kc_target = kc_pos // kc_piece % kc_groups
@@ -251,12 +286,16 @@
             sent, relaid = first_send(src, amplitudes, 64)
         else:
             sent, slab = next_send(src, relaid, slab, 64)
-            slab = lax.all_gather(slab, ("gx", "core"), axis=0, tiled=True)
+            across = [slab] + shifted(slab, "gx")
+            swapped = [shifted(piece, "core")[0] for piece in across]
+            across = across + held_until(swapped)
         arrived = lax.all_to_all(sent.reshape(devices, size * 32, 128), ALL, split_axis=0, concat_axis=0, tiled=True)
         got.append((arrived.reshape(devices * size, 32, 128), got_place[:, start:start + size].reshape(-1)))
         start += size
+    own = jnp.stack([lax.axis_index(name) for name in ("gx", "zhi", "core")]).astype(jnp.int32)
+    whole = [piece.reshape(-1, kc_piece, part, columns) for piece in across]
     for index, (tiles, places) in enumerate(got):
-        acc = products(places, tiles, slab.reshape(planes, -1, part, columns), acc, row_local, index == len(got) - 1)
+        acc = products(places, tiles, whole, own, acc, row_local, index == len(got) - 1)
     shared = lax.all_to_all(
         acc.reshape(kc_groups, row_local // kc_groups * tile_edge, columns), "gz", split_axis=0, concat_axis=0, tiled=True
     )

time: 367 us -> 423 us (1.15)
  waiting for transfers between devices: 60.6 us -> 256 us
  blocking collectives: 218 us -> 46.6 us
  starting transfers between devices: 9.42 us -> 54.2 us
  between operations: 13.5 us -> 0.19 us
    ppermute x0 -> x10, waiting for transfers between devices: none -> 256 us  [shifted(): lax.ppermute(value, axis, [(d, (d + s) % size) for d in range(size)])]
    all_to_all x2 -> x0, blocking collectives: 173 us -> none  [the longest x1 151 us: body(): lax.all_to_all(sent.reshape(devices, size * 32, 128), ALL, split_axis=0,...]
    all_gather x2 -> x0, waiting for transfers between devices: 30.4 us -> none  [the longest x1 30.4 us: body(): slab = lax.all_gather(quarter, 'zhi', axis=0, tiled=True)]
    all_to_all x1 -> x2, waiting for transfers between devices: 30.2 us -> 0.01 us  [body(): lax.all_to_all(sent.reshape(devices, size * 32, 128), ALL, split_axis=0,...]
    all_to_all x1 -> x2, starting transfers between devices: 9.37 us -> 25.1 us  [body(): lax.all_to_all(sent.reshape(devices, size * 32, 128), ALL, split_axis=0,...]
    all_to_all x0 -> x1, starting transfers between devices: none -> 14.7 us  [body(): lax.all_to_all(sent_place, ALL, split_axis=0, concat_axis=0, tiled=True)]
    ppermute x0 -> x10, starting transfers between devices: none -> 14.4 us  [shifted(): lax.ppermute(value, axis, [(d, (d + s) % size) for d in range(size)])]
  transfers between devices with their start and end apart: 3 -> 13, of which waited for: 2 -> 8; matrix products, arithmetic and copies ran while one was open for 2% -> 1% of each run, Pallas kernels for 9% -> 9%
where the time goes in v4:
time: 423 us; the launch traced here: 421 us
  waiting for transfers between devices  256 us (61%)
  starting transfers between devices  54.2 us (13%)
  Pallas kernels  50.3 us (12%)
  blocking collectives  46.6 us (11%)
  local copies, waits for them, and re-layouts  6.74 us (2%)
  other arithmetic  6.52 us (2%)
    ppermute x10, waiting for transfers between devices, shifted(): lax.ppermute(value, axis, [(d, (d + s) % size) for d in range(size)])  256 us
    all_to_all x1, blocking collectives, body(): lax.all_to_all(acc.reshape(kc_groups, row_local // kc_groups * tile_edge,...  46.6 us
    pallas_call x2, Pallas kernels, products(): pl.pallas_call(functools.partial(_product_kernel, has_in, last, block, un...  33.8 us
    all_to_all x2, starting transfers between devices, body(): lax.all_to_all(sent.reshape(devices, size * 32, 128), ALL, split_axis=0,...  25.1 us
    all_to_all x1, starting transfers between devices, body(): lax.all_to_all(sent_place, ALL, split_axis=0, concat_axis=0, tiled=True)  14.7 us
    ppermute x10, starting transfers between devices, shifted(): lax.ppermute(value, axis, [(d, (d + s) % size) for d in range(size)])  14.4 us
    pallas_call x1, Pallas kernels, first_send(): pl.pallas_call(_relayout_kernel, grid_spec=pltpu.PrefetchScalarGridSpec(n...  11.7 us
  transfers between devices with their start and end apart: 13, of which 8 were waited for; matrix products, arithmetic and copies ran while one was open for 1% of the time, Pallas kernels for 9%

profile of v4, /device:TPU:2, one launch (start us, length us, event | category | flops | bytes accessed | tf_op | source)
XLA Modules:
  0.0 420.9 jit_solution(6438304863732740177)
XLA Ops:
  0.0 0.8 and_select_fusion.6
  4.8 14.7 %all-to-all-start = ((s32[256,1,4]{2,1,0:T(1,128)}), s32[256,1,4]{2,1,0:T(1,128)S(1)}, u32[]{:S(2)}, u32[]{:S(2)}) async-start(s32[256,1,4]{2,1,0:T(1,128)} %copy.17), calls=%async_computation | async-start | bytes 262144 | tf_op jit(solution)/shard_map/all_to_all | solution.py:277
  20.5 11.7 %first_send.1 = (bf16[768,32,128]{2,1,0:T(8,128)(2,1)}, bf16[512,32,128]{2,1,0:T(8,128)(2,1)}) custom-call(s32[768]{0:T(1024)} %reshape.177.src_ref, bf16[512,4096]{1,0:T(8,128)(2,1)} %x_ref.1), custom_call_target="tpu_custom_call" | custom-call | tf_op jit(solution)/shard_map/first_send/pallas_call | solution.py:61
  32.1 14.6 %all-to-all-start.2 = ((bf16[256,96,128]{2,1,0:T(8,128)(2,1)}), bf16[256,96,128]{2,1,0:T(8,128)(2,1)}, u32[]{:S(2)}, u32[]{:S(2)}) async-start(bf16[256,96,128]{2,1,0:T(8,128)(2,1)} %bitcast.55), calls=%async_computation.2 | async-start | bytes 12582912 | tf_op jit(solution)/shard_map/all_to_all | solution.py:292
  46.8 5.1 %collective-permute-start.2 = (bf16[800,256]{1,0:T(8,128)(2,1)S(1)}, bf16[800,256]{1,0:T(8,128)(2,1)S(1)}, u32[]{:S(2)}, u32[]{:S(2)}) collective-permute-start(bf16[800,256]{1,0:T(8,128)(2,1)S(1)} %bitcast.57), channel_id=1, source_target_pairs={{0,48},{16,0},{32,16},{48,32},{1,49},{17,1},{33,17},{49,33},{2,50}... | collective-permute-start | bytes 1228808 | tf_op jit(solution)/shard_map/ppermute | solution.py:229
  51.9 1.4 collective-permute-start.1
  53.3 2.8 collective-permute-start
  56.7 148.3 %collective-permute-done.2 = bf16[800,256]{1,0:T(8,128)(2,1)S(1)} collective-permute-done((bf16[800,256]{1,0:T(8,128)(2,1)S(1)}, bf16[800,256]{1,0:T(8,128)(2,1)S(1)}, u32[]{:S(2)}, u32[]{:S(2)}) %collective-permute-start.2) | collective-permute-done | bytes 409632 | tf_op jit(solution)/shard_map/ppermute | solution.py:229
  205.0 4.0 collective-permute-done.1
  209.0 11.2 %collective-permute-done = bf16[800,256]{1,0:T(8,128)(2,1)S(1)} collective-permute-done((bf16[800,256]{1,0:T(8,128)(2,1)S(1)}, bf16[800,256]{1,0:T(8,128)(2,1)S(1)}, u32[]{:S(2)}, u32[]{:S(2)}) %collective-permute-start) | collective-permute-done | bytes 409632 | tf_op jit(solution)/shard_map/ppermute | solution.py:229
  220.1 1.3 pad_maximum_fusion.held_ref
  221.4 4.9 %next_send.1 = (bf16[256,32,128]{2,1,0:T(8,128)(2,1)}, bf16[3200,256]{1,0:T(8,128)(2,1)}) custom-call(s32[256]{0:T(256)} %slice.33.src_ref, bf16[512,32,128]{2,1,0:T(8,128)(2,1)} %get-tuple-element.13.y_ref, bf16[3200,256]{1,0:T(8,128)(2,1)} %pad_maximum_fusion.held_ref), custom_call_target="tpu_custom_call", output_to_operand_aliasing={{1}: (2, {})} | custom-call | tf_op jit(solution)/shard_map/next_send/pallas_call | solution.py:84
  226.3 10.5 %all-to-all-start.1 = ((bf16[256,32,128]{2,1,0:T(8,128)(2,1)}), bf16[256,32,128]{2,1,0:T(8,128)(2,1)}, u32[]{:S(2)}, u32[]{:S(2)}) async-start(bf16[256,32,128]{2,1,0:T(8,128)(2,1)} %get-tuple-element.14), calls=%async_computation.1 | async-start | bytes 4194304 | tf_op jit(solution)/shard_map/all_to_all | solution.py:292
  236.8 2.3 collective-permute-start.5
  239.8 1.8 collective-permute-start.3
  241.6 53.3 %collective-permute-done.5 = bf16[3200,256]{1,0:T(8,128)(2,1)} collective-permute-done((bf16[3200,256]{1,0:T(8,128)(2,1)S(1)}, bf16[3200,256]{1,0:T(8,128)(2,1)}, u32[]{:S(2)}, u32[]{:S(2)}) %collective-permute-start.5) | collective-permute-done | bytes 1638432 | tf_op jit(solution)/shard_map/ppermute | solution.py:229
  294.9 35.4 %collective-permute-done.4 = bf16[3200,256]{1,0:T(8,128)(2,1)} collective-permute-done((bf16[3200,256]{1,0:T(8,128)(2,1)S(1)}, bf16[3200,256]{1,0:T(8,128)(2,1)}, u32[]{:S(2)}, u32[]{:S(2)}) %collective-permute-start.4) | collective-permute-done | bytes 1638432 | tf_op jit(solution)/shard_map/ppermute | solution.py:229
  333.0 1.2 collective-permute-done.8.refs_2_
  334.1 2.3 collective-permute-done.7.refs_1_
  336.5 20.9 %products.2.rest_8_ = f32[104,64,256]{2,1,0:T(8,128)} custom-call(s32[768]{0:T(1024)} %reshape.187.place_ref, s32[3]{0:T(128)} %pad_add_fusion.1.own_ref, bf16[768,32,128]{2,1,0:T(8,128)(2,1)} %bitcast.24.x_hbm, bf16[4,50,16,256]{3,2,1,0:T(8,128)(2,1)} %bitcast.52, bf16[4,50,16,256]{3,2,1,0:T(8,128)(2,1)} %bitcast.16.rest_1_, ...), custom_call_target="tpu_custom_call" | custom-call | tf_op jit(solution)/shard_map/products/pallas_call | solution.py:204
  357.4 12.9 %products.3 = bf16[104,64,256]{2,1,0:T(8,128)(2,1)} custom-call(s32[256]{0:T(256)} %slice_reduce_fusion.place_ref, s32[3]{0:T(128)} %pad_add_fusion.1.own_ref, bf16[256,32,128]{2,1,0:T(8,128)(2,1)} %all-to-all-done.1.x_hbm, bf16[4,50,16,256]{3,2,1,0:T(8,128)(2,1)} %bitcast.53, bf16[4,50,16,256]{3,2,1,0:T(8,128)(2,1)} %bitcast.16.rest_1_, ...), custom_call_target="tpu_custom_call" | custom-call | tf_op jit(solution)/shard_map/products/pallas_call | solution.py:204
  370.3 46.6 %all_to_all.27 = bf16[8,832,256]{2,1,0:T(8,128)(2,1)} all-to-all(bf16[8,832,256]{2,1,0:T(8,128)(2,1)} %bitcast.54), channel_id=1, replica_groups=mesh['gx'=4,'zhi'=4,'core'=2,'gz'=8] {'gz'}, dimensions={0} | all-to-all | bytes 6815744 | tf_op jit(solution)/shard_map/all_to_all | solution.py:299
  416.9 2.6 reduce_sum.52
  420.0 0.9 reshape.192
  (42 shorter events, 9.3 us)
Async XLA Ops:
  0.0 46.7 %copy-start = (bf16[50,64,256]{2,1,0:T(8,128)(2,1)S(1)}, bf16[50,64,256]{2,1,0:T(8,128)(2,1)}, u32[]{:S(2)}) copy-start(bf16[50,64,256]{2,1,0:T(8,128)(2,1)} %param.9) | copy-start | bytes 4915204
  4.8 27.3 %all-to-all-start = ((s32[256,1,4]{2,1,0:T(1,128)}), s32[256,1,4]{2,1,0:T(1,128)S(1)}, u32[]{:S(2)}, u32[]{:S(2)}) async-start(s32[256,1,4]{2,1,0:T(1,128)} %copy.17), calls=%async_computation | async-start | bytes 262144 | tf_op jit(solution)/shard_map/all_to_all | solution.py:277
  32.1 194.2 %all-to-all-start.2 = ((bf16[256,96,128]{2,1,0:T(8,128)(2,1)}), bf16[256,96,128]{2,1,0:T(8,128)(2,1)}, u32[]{:S(2)}, u32[]{:S(2)}) async-start(bf16[256,96,128]{2,1,0:T(8,128)(2,1)} %bitcast.55), calls=%async_computation.2 | async-start | bytes 12582912 | tf_op jit(solution)/shard_map/all_to_all | solution.py:292
  46.8 158.2 %collective-permute-start.2 = (bf16[800,256]{1,0:T(8,128)(2,1)S(1)}, bf16[800,256]{1,0:T(8,128)(2,1)S(1)}, u32[]{:S(2)}, u32[]{:S(2)}) collective-permute-start(bf16[800,256]{1,0:T(8,128)(2,1)S(1)} %bitcast.57), channel_id=1, source_target_pairs={{0,48},{16,0},{32,16},{48,32},{1,49},{17,1},{33,17},{49,33},{2,50}... | collective-permute-start | bytes 1228808 | tf_op jit(solution)/shard_map/ppermute | solution.py:229
  51.9 157.1 %collective-permute-start.1 = (bf16[800,256]{1,0:T(8,128)(2,1)S(1)}, bf16[800,256]{1,0:T(8,128)(2,1)S(1)}, u32[]{:S(2)}, u32[]{:S(2)}) collective-permute-start(bf16[800,256]{1,0:T(8,128)(2,1)S(1)} %bitcast.58), channel_id=1, source_target_pairs={{0,32},{16,48},{32,0},{48,16},{1,33},{17,49},{33,1},{49,17},{2,34}... | collective-permute-start | bytes 1228808 | tf_op jit(solution)/shard_map/ppermute | solution.py:229
  53.3 166.9 %collective-permute-start = (bf16[800,256]{1,0:T(8,128)(2,1)S(1)}, bf16[800,256]{1,0:T(8,128)(2,1)S(1)}, u32[]{:S(2)}, u32[]{:S(2)}) collective-permute-start(bf16[800,256]{1,0:T(8,128)(2,1)S(1)} %bitcast.59), channel_id=1, source_target_pairs={{0,16},{16,32},{32,48},{48,0},{1,17},{17,33},{33,49},{49,1},{2,18}... | collective-permute-start | bytes 1228808 | tf_op jit(solution)/shard_map/ppermute | solution.py:229
  226.3 10.5 %copy-start.1 = (bf16[3200,256]{1,0:T(8,128)(2,1)S(1)}, bf16[3200,256]{1,0:T(8,128)(2,1)}, u32[]{:S(2)}) copy-start(bf16[3200,256]{1,0:T(8,128)(2,1)} %get-tuple-element.15) | copy-start | bytes 4915204
  226.3 131.1 %all-to-all-start.1 = ((bf16[256,32,128]{2,1,0:T(8,128)(2,1)}), bf16[256,32,128]{2,1,0:T(8,128)(2,1)}, u32[]{:S(2)}, u32[]{:S(2)}) async-start(bf16[256,32,128]{2,1,0:T(8,128)(2,1)} %get-tuple-element.14), calls=%async_computation.1 | async-start | bytes 4194304 | tf_op jit(solution)/shard_map/all_to_all | solution.py:292
  236.8 58.1 %collective-permute-start.5 = (bf16[3200,256]{1,0:T(8,128)(2,1)S(1)}, bf16[3200,256]{1,0:T(8,128)(2,1)}, u32[]{:S(2)}, u32[]{:S(2)}) collective-permute-start(bf16[3200,256]{1,0:T(8,128)(2,1)S(1)} %copy-done.1), channel_id=1, source_target_pairs={{0,192},{64,0},{128,64},{192,128},{1,193},{65,1},{129,65},{193,129... | collective-permute-start | bytes 4915208 | tf_op jit(solution)/shard_map/ppermute | solution.py:229
  239.1 91.2 %collective-permute-start.4 = (bf16[3200,256]{1,0:T(8,128)(2,1)S(1)}, bf16[3200,256]{1,0:T(8,128)(2,1)}, u32[]{:S(2)}, u32[]{:S(2)}) collective-permute-start(bf16[3200,256]{1,0:T(8,128)(2,1)S(1)} %copy-done.1), channel_id=1, source_target_pairs={{0,128},{64,192},{128,0},{192,64},{1,129},{65,193},{129,1},{193,65... | collective-permute-start | bytes 4915208 | tf_op jit(solution)/shard_map/ppermute | solution.py:229
  239.8 90.7 %collective-permute-start.3 = (bf16[3200,256]{1,0:T(8,128)(2,1)S(1)}, bf16[3200,256]{1,0:T(8,128)(2,1)}, u32[]{:S(2)}, u32[]{:S(2)}) collective-permute-start(bf16[3200,256]{1,0:T(8,128)(2,1)S(1)} %copy-done.1), channel_id=1, source_target_pairs={{0,64},{64,128},{128,192},{192,0},{1,65},{65,129},{129,193},{193,1... | collective-permute-start | bytes 4915208 | tf_op jit(solution)/shard_map/ppermute | solution.py:229
  241.6 91.4 %collective-permute-start.6 = (bf16[3200,256]{1,0:T(8,128)(2,1)S(1)}, bf16[3200,256]{1,0:T(8,128)(2,1)}, u32[]{:S(2)}, u32[]{:S(2)}) collective-permute-start(bf16[3200,256]{1,0:T(8,128)(2,1)S(1)} %copy-done.1), channel_id=1, source_target_pairs={{0,8},{8,0},{1,9},{9,1},{2,10},{10,2},{3,11},{11,3},{4,12},{12,4},... | collective-permute-start | bytes 4915208 | tf_op jit(solution)/shard_map/ppermute | solution.py:229
  294.9 38.1 %collective-permute-start.9 = (bf16[3200,256]{1,0:T(8,128)(2,1)}, bf16[3200,256]{1,0:T(8,128)(2,1)}, u32[]{:S(2)}, u32[]{:S(2)}) collective-permute-start(bf16[3200,256]{1,0:T(8,128)(2,1)} %collective-permute-done.5), channel_id=1, source_target_pairs={{0,8},{8,0},{1,9},{9,1},{2,10},{10,2},{3,11},{11,3},{4,12},{12,4},... | collective-permute-start | bytes 4915208 | tf_op jit(solution)/shard_map/ppermute | solution.py:229
  330.3 3.8 collective-permute-start.8
  330.5 6.0 %collective-permute-start.7 = (bf16[3200,256]{1,0:T(8,128)(2,1)}, bf16[3200,256]{1,0:T(8,128)(2,1)}, u32[]{:S(2)}, u32[]{:S(2)}) collective-permute-start(bf16[3200,256]{1,0:T(8,128)(2,1)} %collective-permute-done.3), channel_id=1, source_target_pairs={{0,8},{8,0},{1,9},{9,1},{2,10},{10,2},{3,11},{11,3},{4,12},{12,4},... | collective-permute-start | bytes 4915208 | tf_op jit(solution)/shard_map/ppermute | solution.py:229

commit v5 on v4

--- a/solution.py
+++ b/solution.py
@@ -15,10 +15,14 @@
 VMEM_LIMIT = 62 * 1024 * 1024
 
 
-def _relayout_kernel(src_ref, x_ref, out_ref, y_ref, *tmps):
+def _relayout_kernel(src_ref, place_ref, x_ref, out_ref, y_ref, *tmps):
     tiles = x_ref.shape[0]
     q_rows = x_ref.shape[1] // 128
     group = 8 * len(tmps)
+    block, rows, _ = out_ref.shape
+    taken = rows // q_rows
+    devices = src_ref.shape[0] // taken
+    base = pl.program_id(0) * block
 
     @pl.when(pl.program_id(0) == 0)
     def _():
@@ -34,7 +38,25 @@
 
         lax.fori_loop(0, tiles // group, one, 0)
 
-    _copy_slots(src_ref, y_ref, out_ref)
+    lane = lax.broadcasted_iota(jnp.int32, (8, 128), 1)
+    slot = lane % CAP
+
+    def send(g, carry):
+        for u in range(8):
+            d = g * 8 + u
+            for k in range(taken):
+                out_ref[d, pl.ds(k * q_rows, q_rows), :] = y_ref[src_ref[k * devices + base + d]]
+            value = jnp.full((8, 128), place_ref[base + d], jnp.int32)
+            for k in range(1, CAP):
+                value = jnp.where(slot == k, place_ref[k * devices + base + d], value)
+            high = lax.shift_right_logical(value, 10)
+            middle = lax.bitwise_and(lax.shift_right_logical(value, 5), 31)
+            low = lax.bitwise_and(value, 31)
+            field = jnp.where(lane < CAP, high, jnp.where(lane < 2 * CAP, middle, low))
+            out_ref[d, pl.ds(taken * q_rows, 8), :] = field.astype(jnp.float32).astype(out_ref.dtype)
+        return carry
+
+    lax.fori_loop(0, block // 8, send, 0)
 
 
 def _copy_slots(src_ref, y_ref, out_ref):
@@ -54,29 +76,30 @@
     _copy_slots(src_ref, y_ref, out_ref)
 
 
-def first_send(src, x, block):
+def first_send(src, place, x, taken, block):
     tiles, width = x.shape
     q_rows = width // 128
-    slots = src.shape[0]
+    devices = src.shape[0] // taken
+    rows = taken * q_rows + 8
     return pl.pallas_call(
         _relayout_kernel,
         grid_spec=pltpu.PrefetchScalarGridSpec(
-            num_scalar_prefetch=1,
-            grid=(slots // block,),
-            in_specs=[pl.BlockSpec((tiles, width), lambda i, s: (0, 0))],
+            num_scalar_prefetch=2,
+            grid=(devices // block,),
+            in_specs=[pl.BlockSpec((tiles, width), lambda i, s, p: (0, 0))],
             out_specs=[
-                pl.BlockSpec((block, q_rows, 128), lambda i, s: (i, 0, 0)),
-                pl.BlockSpec((tiles, q_rows, 128), lambda i, s: (0, 0, 0)),
+                pl.BlockSpec((block, rows, 128), lambda i, s, p: (i, 0, 0)),
+                pl.BlockSpec((tiles, q_rows, 128), lambda i, s, p: (0, 0, 0)),
             ],
             scratch_shapes=[pltpu.VMEM((8 * q_rows, 128), jnp.float32) for _ in range(RELAYOUT)],
         ),
         out_shape=[
-            jax.ShapeDtypeStruct((slots, q_rows, 128), x.dtype),
+            jax.ShapeDtypeStruct((devices, rows, 128), x.dtype),
             jax.ShapeDtypeStruct((tiles, q_rows, 128), x.dtype),
         ],
         compiler_params=pltpu.CompilerParams(vmem_limit_bytes=VMEM_LIMIT),
         name="first_send",
-    )(src, x)
+    )(src, place, x)
 
 
 def next_send(src, y, held, block):
@@ -121,7 +144,7 @@
     )(*values))
 
 
-def _product_kernel(has_in, last, block, unroll, place_ref, own_ref, x_hbm, *rest):
+def _product_kernel(has_in, last, block, unroll, start, taken, place_ref, own_ref, x_hbm, *rest):
     parts, rest = rest[:8], rest[8:]
     if has_in:
         acc_in, out_hbm, acc, w_ref, prod, xbuf, before, held, w_sem, x_sem, sem = rest
@@ -163,17 +186,17 @@
 
         def group(i, carry):
             where = []
-            for u in range(unroll):
-                n = i * unroll + u
-                v = place_ref[b * block + n]
+            for t in range(unroll * taken):
+                n, k = i * unroll + t // taken, t % taken
+                v = place_ref[(b * block + n) * CAP + start + k]
                 where.append(lax.shift_right_logical(v, 10))
                 kc = lax.bitwise_and(v, 1023)
-                p = xbuf[slot, n]
+                p = xbuf[slot, n, pl.ds(k * 32, 32), :]
                 a = jnp.concatenate([p[:, :64], p[:, 64:]], axis=0)
-                w = jnp.concatenate([w_ref[k, kc] for k in range(4)], axis=0)
-                prod[u] = jnp.dot(a, w, preferred_element_type=jnp.float32)
-            for u in range(unroll):
-                acc[where[u]] += prod[u]
+                w = jnp.concatenate([w_ref[q, kc] for q in range(4)], axis=0)
+                prod[t] = jnp.dot(a, w, preferred_element_type=jnp.float32)
+            for t in range(unroll * taken):
+                acc[where[t]] += prod[t]
             return carry
 
         lax.fori_loop(0, block // unroll, group, 0)
@@ -195,21 +218,21 @@
     away.wait()
 
 
-def products(place, x, parts, own, acc_in, row_local, last, block=128, unroll=32):
+def products(place, x, parts, own, acc_in, row_local, last, start, taken, block, unroll):
     has_in = acc_in is not None
     operands = (place, own, x, *parts) + ((acc_in,) if has_in else ())
     group, piece, rows, columns = parts[0].shape
     edge = rows * group
     result = jax.ShapeDtypeStruct((row_local, edge, columns), jnp.bfloat16 if last else jnp.float32)
     return pl.pallas_call(
-        functools.partial(_product_kernel, has_in, last, block, unroll),
+        functools.partial(_product_kernel, has_in, last, block, unroll, start, taken),
         in_specs=[pl.BlockSpec(memory_space=pltpu.SMEM)] * 2 + [pl.BlockSpec(memory_space=pl.ANY)] * (len(operands) - 2),
         out_specs=pl.BlockSpec(memory_space=pl.ANY),
         scratch_shapes=[
             pltpu.VMEM((row_local + 1, edge, columns), jnp.float32),
             pltpu.VMEM((4, 2 * group * piece, rows, columns), x.dtype),
-            pltpu.VMEM((unroll, edge, columns), jnp.float32),
-            pltpu.VMEM((2, block, 32, 128), x.dtype),
+            pltpu.VMEM((unroll * taken, edge, columns), jnp.float32),
+            pltpu.VMEM((2, block) + x.shape[1:], x.dtype),
         ] + ([
             pltpu.VMEM((row_local, edge, columns), jnp.float32),
             pltpu.VMEM(result.shape, result.dtype),
@@ -273,29 +296,31 @@
     empty = row_local * 1024
     sent_place = empty + jnp.sum(jnp.where(matches, place[None, :] - empty, 0), axis=1)
     source = source.reshape(CAP, devices)
-    sent_place = sent_place.reshape(CAP, devices).T
-    got_place = lax.all_to_all(sent_place, ALL, split_axis=0, concat_axis=0, tiled=True)
-
     acc = None
     start = 0
     relaid = None
     got = []
     for size in CHUNKS:
-        src = source[start:start + size].T.reshape(-1)
+        src = source[start:start + size].reshape(-1)
         if relaid is None:
-            sent, relaid = first_send(src, amplitudes, 64)
+            sent, relaid = first_send(src, sent_place, amplitudes, size, 32)
         else:
             sent, slab = next_send(src, relaid, slab, 64)
             across = [slab] + shifted(slab, "gx")
             swapped = [shifted(piece, "core")[0] for piece in across]
             across = across + held_until(swapped)
-        arrived = lax.all_to_all(sent.reshape(devices, size * 32, 128), ALL, split_axis=0, concat_axis=0, tiled=True)
-        got.append((arrived.reshape(devices * size, 32, 128), got_place[:, start:start + size].reshape(-1)))
+        arrived = lax.all_to_all(sent, ALL, split_axis=0, concat_axis=0, tiled=True)
+        got.append((arrived, start, size))
         start += size
+    fields = got[0][0][:, 32 * CHUNKS[0], :3 * CAP].astype(jnp.int32)
+    places = (fields[:, :CAP] * 1024 + fields[:, CAP:2 * CAP] * 32 + fields[:, 2 * CAP:]).reshape(-1)
     own = jnp.stack([lax.axis_index(name) for name in ("gx", "zhi", "core")]).astype(jnp.int32)
     whole = [piece.reshape(-1, kc_piece, part, columns) for piece in across]
-    for index, (tiles, places) in enumerate(got):
-        acc = products(places, tiles, whole, own, acc, row_local, index == len(got) - 1)
+    for index, (tiles, start, size) in enumerate(got):
+        last = index == len(got) - 1
+        acc = products(
+            places, tiles, whole, own, acc, row_local, last, start, size, 32 if size > 1 else 64, 8 if size > 1 else 32
+        )
     shared = lax.all_to_all(
         acc.reshape(kc_groups, row_local // kc_groups * tile_edge, columns), "gz", split_axis=0, concat_axis=0, tiled=True
     )

time: 423 us -> 423 us (level)
  starting transfers between devices: 54.2 us -> 40.5 us
  waiting for transfers between devices: 256 us -> 268 us
    all_to_all x3 -> x2, starting transfers between devices: 39.8 us -> 26.1 us  [body(): arrived = lax.all_to_all(sent, ALL, split_axis=0, concat_axis=0, tiled=True)]
    ppermute x10, waiting for transfers between devices: 256 us -> 268 us  [shifted(): lax.ppermute(value, axis, [(d, (d + s) % size) for d in range(size)])]
  transfers between devices with their start and end apart: 13 -> 12, of which waited for: 8 -> 8; matrix products, arithmetic and copies ran while one was open for 1% -> 1% of each run, Pallas kernels for 9% -> 6%
where the time goes in v5:
time: 423 us; the launch traced here: 421 us
  waiting for transfers between devices  268 us (63%)
  Pallas kernels  51.8 us (12%)
  blocking collectives  46.5 us (11%)
  starting transfers between devices  40.5 us (10%)
  other arithmetic  8.93 us (2%)
  local copies, waits for them, and re-layouts  4.85 us (1%)
    ppermute x10, waiting for transfers between devices, shifted(): lax.ppermute(value, axis, [(d, (d + s) % size) for d in range(size)])  268 us
    all_to_all x1, blocking collectives, body(): lax.all_to_all(acc.reshape(kc_groups, row_local // kc_groups * tile_edge,...  46.5 us
    pallas_call x2, Pallas kernels, products(): pl.pallas_call(functools.partial(_product_kernel, has_in, last, block, un...  36 us
    all_to_all x2, starting transfers between devices, body(): arrived = lax.all_to_all(sent, ALL, split_axis=0, concat_axis=0, tiled=True)  26.1 us
    ppermute x10, starting transfers between devices, shifted(): lax.ppermute(value, axis, [(d, (d + s) % size) for d in range(size)])  14.4 us
    pallas_call x1, Pallas kernels, first_send(): pl.pallas_call(_relayout_kernel, grid_spec=pltpu.PrefetchScalarGridSpec(n...  10.9 us
  transfers between devices with their start and end apart: 12, of which 8 were waited for; matrix products, arithmetic and copies ran while one was open for 1% of the time, Pallas kernels for 6%

profile of v5, /device:TPU:2, one launch (start us, length us, event | category | flops | bytes accessed | tf_op | source)
XLA Modules:
  0.0 421.3 jit_solution(13847600515323882412)
XLA Ops:
  3.3 1.2 select_reduce_fusion
  5.1 10.9 %first_send.1 = (bf16[256,104,128]{2,1,0:T(8,128)(2,1)}, bf16[512,32,128]{2,1,0:T(8,128)(2,1)}) custom-call(s32[768]{0:T(1024)} %bitcast.54, s32[1024]{0:T(1024)} %broadcast_add_fusion.place_ref, bf16[512,4096]{1,0:T(8,128)(2,1)} %x_ref.1), custom_call_target="tpu_custom_call" | custom-call | tf_op jit(solution)/shard_map/first_send/pallas_call | solution.py:84
  16.0 15.6 %all-to-all-start = ((bf16[256,104,128]{2,1,0:T(8,128)(2,1)}), bf16[256,104,128]{2,1,0:T(8,128)(2,1)}, u32[]{:S(2)}, u32[]{:S(2)}) async-start(bf16[256,104,128]{2,1,0:T(8,128)(2,1)} %get-tuple-element.13), calls=%async_computation | async-start | bytes 13631488 | tf_op jit(solution)/shard_map/all_to_all | solution.py:312
  31.7 5.1 %collective-permute-start.2 = (bf16[800,256]{1,0:T(8,128)(2,1)S(1)}, bf16[800,256]{1,0:T(8,128)(2,1)S(1)}, u32[]{:S(2)}, u32[]{:S(2)}) collective-permute-start(bf16[800,256]{1,0:T(8,128)(2,1)S(1)} %bitcast.50), channel_id=1, source_target_pairs={{0,48},{16,0},{32,16},{48,32},{1,49},{17,1},{33,17},{49,33},{2,50}... | collective-permute-start | bytes 1228808 | tf_op jit(solution)/shard_map/ppermute | solution.py:252
  36.8 1.4 collective-permute-start.1
  38.1 2.8 collective-permute-start
  41.0 1.3 slice.33.src_ref
  42.2 159.1 %collective-permute-done.2 = bf16[800,256]{1,0:T(8,128)(2,1)S(1)} collective-permute-done((bf16[800,256]{1,0:T(8,128)(2,1)S(1)}, bf16[800,256]{1,0:T(8,128)(2,1)S(1)}, u32[]{:S(2)}, u32[]{:S(2)}) %collective-permute-start.2) | collective-permute-done | bytes 409632 | tf_op jit(solution)/shard_map/ppermute | solution.py:252
  201.3 3.1 collective-permute-done.1
  204.4 11.9 %collective-permute-done = bf16[800,256]{1,0:T(8,128)(2,1)S(1)} collective-permute-done((bf16[800,256]{1,0:T(8,128)(2,1)S(1)}, bf16[800,256]{1,0:T(8,128)(2,1)S(1)}, u32[]{:S(2)}, u32[]{:S(2)}) %collective-permute-start) | collective-permute-done | bytes 409632 | tf_op jit(solution)/shard_map/ppermute | solution.py:252
  216.2 1.3 pad_maximum_fusion.held_ref
  217.5 4.9 %next_send.1 = (bf16[256,32,128]{2,1,0:T(8,128)(2,1)}, bf16[3200,256]{1,0:T(8,128)(2,1)}) custom-call(s32[256]{0:T(256)} %slice.33.src_ref, bf16[512,32,128]{2,1,0:T(8,128)(2,1)} %get-tuple-element.14.y_ref, bf16[3200,256]{1,0:T(8,128)(2,1)} %pad_maximum_fusion.held_ref), custom_call_target="tpu_custom_call", output_to_operand_aliasing={{1}: (2, {})} | custom-call | tf_op jit(solution)/shard_map/next_send/pallas_call | solution.py:107
  222.5 10.5 %all-to-all-start.1 = ((bf16[256,32,128]{2,1,0:T(8,128)(2,1)}), bf16[256,32,128]{2,1,0:T(8,128)(2,1)}, u32[]{:S(2)}, u32[]{:S(2)}) async-start(bf16[256,32,128]{2,1,0:T(8,128)(2,1)} %get-tuple-element.15), calls=%async_computation.1 | async-start | bytes 4194304 | tf_op jit(solution)/shard_map/all_to_all | solution.py:312
  233.0 2.3 collective-permute-start.5
  236.0 1.8 collective-permute-start.3
  237.8 53.3 %collective-permute-done.5 = bf16[3200,256]{1,0:T(8,128)(2,1)} collective-permute-done((bf16[3200,256]{1,0:T(8,128)(2,1)S(1)}, bf16[3200,256]{1,0:T(8,128)(2,1)}, u32[]{:S(2)}, u32[]{:S(2)}) %collective-permute-start.5) | collective-permute-done | bytes 1638432 | tf_op jit(solution)/shard_map/ppermute | solution.py:252
  291.1 35.4 %collective-permute-done.4 = bf16[3200,256]{1,0:T(8,128)(2,1)} collective-permute-done((bf16[3200,256]{1,0:T(8,128)(2,1)S(1)}, bf16[3200,256]{1,0:T(8,128)(2,1)}, u32[]{:S(2)}, u32[]{:S(2)}) %collective-permute-start.4) | collective-permute-done | bytes 1638432 | tf_op jit(solution)/shard_map/ppermute | solution.py:252
  327.6 2.7 collective-permute-done.8.refs_2_
  330.3 2.3 collective-permute-done.7.refs_1_
  332.7 1.1 slice_convert_fusion
  334.7 22.4 %products.2.rest_8_ = f32[104,64,256]{2,1,0:T(8,128)} custom-call(s32[1024]{0:T(1024)} %reshape.155.place_ref, s32[3]{0:T(128)} %pad_add_fusion.1.own_ref, bf16[256,104,128]{2,1,0:T(8,128)(2,1)} %all-to-all-done.x_hbm, bf16[4,50,16,256]{3,2,1,0:T(8,128)(2,1)} %bitcast.45, bf16[4,50,16,256]{3,2,1,0:T(8,128)(2,1)} %bitcast.13.rest_1_, ...), custom_call_target="tpu_custom_call" | custom-call | tf_op jit(solution)/shard_map/products/pallas_call | solution.py:227
  357.0 13.6 %products.3 = bf16[104,64,256]{2,1,0:T(8,128)(2,1)} custom-call(s32[1024]{0:T(1024)} %reshape.155.place_ref, s32[3]{0:T(128)} %pad_add_fusion.1.own_ref, bf16[256,32,128]{2,1,0:T(8,128)(2,1)} %all-to-all-done.1.x_hbm, bf16[4,50,16,256]{3,2,1,0:T(8,128)(2,1)} %bitcast.46, bf16[4,50,16,256]{3,2,1,0:T(8,128)(2,1)} %bitcast.13.rest_1_, ...), custom_call_target="tpu_custom_call" | custom-call | tf_op jit(solution)/shard_map/products/pallas_call | solution.py:227
  370.7 46.5 %all_to_all.15 = bf16[8,832,256]{2,1,0:T(8,128)(2,1)} all-to-all(bf16[8,832,256]{2,1,0:T(8,128)(2,1)} %bitcast.47), channel_id=1, replica_groups=mesh['gx'=4,'zhi'=4,'core'=2,'gz'=8] {'gz'}, dimensions={0} | all-to-all | bytes 6815744 | tf_op jit(solution)/shard_map/all_to_all | solution.py:324
  417.2 2.6 reduce_sum.52
  (36 shorter events, 7.9 us)
Async XLA Ops:
  0.0 31.6 %copy-start = (bf16[50,64,256]{2,1,0:T(8,128)(2,1)S(1)}, bf16[50,64,256]{2,1,0:T(8,128)(2,1)}, u32[]{:S(2)}) copy-start(bf16[50,64,256]{2,1,0:T(8,128)(2,1)} %param.9) | copy-start | bytes 4915204
  16.0 206.4 %all-to-all-start = ((bf16[256,104,128]{2,1,0:T(8,128)(2,1)}), bf16[256,104,128]{2,1,0:T(8,128)(2,1)}, u32[]{:S(2)}, u32[]{:S(2)}) async-start(bf16[256,104,128]{2,1,0:T(8,128)(2,1)} %get-tuple-element.13), calls=%async_computation | async-start | bytes 13631488 | tf_op jit(solution)/shard_map/all_to_all | solution.py:312
  31.7 169.6 %collective-permute-start.2 = (bf16[800,256]{1,0:T(8,128)(2,1)S(1)}, bf16[800,256]{1,0:T(8,128)(2,1)S(1)}, u32[]{:S(2)}, u32[]{:S(2)}) collective-permute-start(bf16[800,256]{1,0:T(8,128)(2,1)S(1)} %bitcast.50), channel_id=1, source_target_pairs={{0,48},{16,0},{32,16},{48,32},{1,49},{17,1},{33,17},{49,33},{2,50}... | collective-permute-start | bytes 1228808 | tf_op jit(solution)/shard_map/ppermute | solution.py:252
  36.8 167.6 %collective-permute-start.1 = (bf16[800,256]{1,0:T(8,128)(2,1)S(1)}, bf16[800,256]{1,0:T(8,128)(2,1)S(1)}, u32[]{:S(2)}, u32[]{:S(2)}) collective-permute-start(bf16[800,256]{1,0:T(8,128)(2,1)S(1)} %bitcast.51), channel_id=1, source_target_pairs={{0,32},{16,48},{32,0},{48,16},{1,33},{17,49},{33,1},{49,17},{2,34}... | collective-permute-start | bytes 1228808 | tf_op jit(solution)/shard_map/ppermute | solution.py:252
  38.1 178.1 %collective-permute-start = (bf16[800,256]{1,0:T(8,128)(2,1)S(1)}, bf16[800,256]{1,0:T(8,128)(2,1)S(1)}, u32[]{:S(2)}, u32[]{:S(2)}) collective-permute-start(bf16[800,256]{1,0:T(8,128)(2,1)S(1)} %bitcast.52), channel_id=1, source_target_pairs={{0,16},{16,32},{32,48},{48,0},{1,17},{17,33},{33,49},{49,1},{2,18}... | collective-permute-start | bytes 1228808 | tf_op jit(solution)/shard_map/ppermute | solution.py:252
  222.5 10.5 %copy-start.1 = (bf16[3200,256]{1,0:T(8,128)(2,1)S(1)}, bf16[3200,256]{1,0:T(8,128)(2,1)}, u32[]{:S(2)}) copy-start(bf16[3200,256]{1,0:T(8,128)(2,1)} %get-tuple-element.16) | copy-start | bytes 4915204
  222.5 134.6 %all-to-all-start.1 = ((bf16[256,32,128]{2,1,0:T(8,128)(2,1)}), bf16[256,32,128]{2,1,0:T(8,128)(2,1)}, u32[]{:S(2)}, u32[]{:S(2)}) async-start(bf16[256,32,128]{2,1,0:T(8,128)(2,1)} %get-tuple-element.15), calls=%async_computation.1 | async-start | bytes 4194304 | tf_op jit(solution)/shard_map/all_to_all | solution.py:312
  233.0 58.1 %collective-permute-start.5 = (bf16[3200,256]{1,0:T(8,128)(2,1)S(1)}, bf16[3200,256]{1,0:T(8,128)(2,1)}, u32[]{:S(2)}, u32[]{:S(2)}) collective-permute-start(bf16[3200,256]{1,0:T(8,128)(2,1)S(1)} %copy-done.1), channel_id=1, source_target_pairs={{0,192},{64,0},{128,64},{192,128},{1,193},{65,1},{129,65},{193,129... | collective-permute-start | bytes 4915208 | tf_op jit(solution)/shard_map/ppermute | solution.py:252
  235.3 91.2 %collective-permute-start.4 = (bf16[3200,256]{1,0:T(8,128)(2,1)S(1)}, bf16[3200,256]{1,0:T(8,128)(2,1)}, u32[]{:S(2)}, u32[]{:S(2)}) collective-permute-start(bf16[3200,256]{1,0:T(8,128)(2,1)S(1)} %copy-done.1), channel_id=1, source_target_pairs={{0,128},{64,192},{128,0},{192,64},{1,129},{65,193},{129,1},{193,65... | collective-permute-start | bytes 4915208 | tf_op jit(solution)/shard_map/ppermute | solution.py:252
  236.0 90.7 %collective-permute-start.3 = (bf16[3200,256]{1,0:T(8,128)(2,1)S(1)}, bf16[3200,256]{1,0:T(8,128)(2,1)}, u32[]{:S(2)}, u32[]{:S(2)}) collective-permute-start(bf16[3200,256]{1,0:T(8,128)(2,1)S(1)} %copy-done.1), channel_id=1, source_target_pairs={{0,64},{64,128},{128,192},{192,0},{1,65},{65,129},{129,193},{193,1... | collective-permute-start | bytes 4915208 | tf_op jit(solution)/shard_map/ppermute | solution.py:252
  237.8 89.9 %collective-permute-start.6 = (bf16[3200,256]{1,0:T(8,128)(2,1)S(1)}, bf16[3200,256]{1,0:T(8,128)(2,1)}, u32[]{:S(2)}, u32[]{:S(2)}) collective-permute-start(bf16[3200,256]{1,0:T(8,128)(2,1)S(1)} %copy-done.1), channel_id=1, source_target_pairs={{0,8},{8,0},{1,9},{9,1},{2,10},{10,2},{3,11},{11,3},{4,12},{12,4},... | collective-permute-start | bytes 4915208 | tf_op jit(solution)/shard_map/ppermute | solution.py:252
  291.1 36.6 %collective-permute-start.9 = (bf16[3200,256]{1,0:T(8,128)(2,1)}, bf16[3200,256]{1,0:T(8,128)(2,1)}, u32[]{:S(2)}, u32[]{:S(2)}) collective-permute-start(bf16[3200,256]{1,0:T(8,128)(2,1)} %collective-permute-done.5), channel_id=1, source_target_pairs={{0,8},{8,0},{1,9},{9,1},{2,10},{10,2},{3,11},{11,3},{4,12},{12,4},... | collective-permute-start | bytes 4915208 | tf_op jit(solution)/shard_map/ppermute | solution.py:252
  326.5 3.8 collective-permute-start.8
  326.7 6.0 %collective-permute-start.7 = (bf16[3200,256]{1,0:T(8,128)(2,1)}, bf16[3200,256]{1,0:T(8,128)(2,1)}, u32[]{:S(2)}, u32[]{:S(2)}) collective-permute-start(bf16[3200,256]{1,0:T(8,128)(2,1)} %collective-permute-done.3), channel_id=1, source_target_pairs={{0,8},{8,0},{1,9},{9,1},{2,10},{10,2},{3,11},{11,3},{4,12},{12,4},... | collective-permute-start | bytes 4915208 | tf_op jit(solution)/shard_map/ppermute | solution.py:252
